TPU v7x, 32 devices: a whole 2x2x4 slice. The times are simulated.
32 devices in a mesh: dp: 8 (over z, y), tensor: 4 (over x, core).
Axes of the slice: x: 2, y: 2, z: 4, core: 2. Of those that a mesh axis runs over, the one named last changes fastest.
Arguments:
- tokens: bfloat16 [16384, 512], P(('dp', 'tensor')), may hold values from -6 to 6
- encoder_states: bfloat16 [16384, 512], P(('dp', 'tensor')), may hold values from -6 to 6
- output_grad: bfloat16 [16384, 512], P(('dp', 'tensor')), may hold values from -6 to 6
- valid_mask: int32 [16384], P(('dp', 'tensor')), may hold values 0 or 1
- segment_ids: int32 [16, 1024], P('dp'), may hold values from 0 to 15, never falling along the last dimension, each value on 1 to 512 neighbouring positions
- context_ranks: int32 [16, 8], P('dp'), may hold values from 0 to 7, each once within a row
- self_query: bfloat16 [512, 512], P('dp', 'tensor'), may hold values from -0.25 to 0.25
- self_key: bfloat16 [512, 512], P('dp', 'tensor'), may hold values from -0.25 to 0.25
- self_value: bfloat16 [512, 512], P('dp', 'tensor'), may hold values from -0.25 to 0.25
- self_output: bfloat16 [512, 512], P('tensor', 'dp'), may hold values from -1.5 to 1.5
- cross_query: bfloat16 [512, 512], P('dp', 'tensor'), may hold values from -0.25 to 0.25
- cross_key: bfloat16 [512, 512], P('dp', 'tensor'), may hold values from -0.25 to 0.25
- cross_value: bfloat16 [512, 512], P('dp', 'tensor'), may hold values from -0.25 to 0.25
- cross_output: bfloat16 [512, 512], P('tensor', 'dp'), may hold values from -4 to 4
- hidden_up: bfloat16 [512, 2048], P('dp', 'tensor'), may hold values from -0.25 to 0.25
- hidden_down: bfloat16 [2048, 512], P('tensor', 'dp'), may hold values from -0.1875 to 0.1875
- norm1_gain: float32 [512], replicated, may hold values from 0.5 to 1.5
- norm1_bias: float32 [512], replicated, may hold values from -1.2 to 1.2
- norm2_gain: float32 [512], replicated, may hold values from 0.5 to 1.5
- norm2_bias: float32 [512], replicated, may hold values from -1.2 to 1.2
- norm3_gain: float32 [512], replicated, may hold values from 0.5 to 1.5
- norm3_bias: float32 [512], replicated, may hold values from -1.2 to 1.2
Outputs:
- layer_output: float32 [16384, 512], P(('dp', 'tensor'))
- tokens_grad: float32 [16384, 512], P(('dp', 'tensor'))
- encoder_grad: float32 [16384, 512], P(('dp', 'tensor'))
- grad_self_query: float32 [512, 512], P('dp', 'tensor')
- grad_self_key: float32 [512, 512], P('dp', 'tensor')
- grad_self_value: float32 [512, 512], P('dp', 'tensor')
- grad_self_output: float32 [512, 512], P('tensor', 'dp')
- grad_cross_query: float32 [512, 512], P('dp', 'tensor')
- grad_cross_key: float32 [512, 512], P('dp', 'tensor')
- grad_cross_value: float32 [512, 512], P('dp', 'tensor')
- grad_cross_output: float32 [512, 512], P('tensor', 'dp')
- grad_hidden_up: float32 [512, 2048], P('dp', 'tensor')
- grad_hidden_down: float32 [2048, 512], P('tensor', 'dp')
- norm_grads: float32 [6, 512], replicated
- valid_scales: float32 [2, 512], replicated
Inputs may be any that keep to these rules, and one draw needn't show every extreme that they name: `segment_ids`: within a sequence the ids never fall; each document has 1 to 512 tokens and one has exactly 512. `context_ranks`: each sequence's row holds every block rank once.
All inputs are finite; a program needn't handle non-finite values. No bound on the sum of `valid_mask` on one device may be relied on, other than what follows from the above.
Results may differ from a plain program's by a relative error of at most 0.024.
The roundings to bfloat16 on the way count: a program that leaves them out, or rounds other values in their place, can miss the bound.
Values may be sent and summed in bfloat16 or wider, within the bound.
A program may use at most 128 MiB of HBM per device.

v0:
```python
import jax
import jax.numpy as jnp
from jax import lax
from jax.sharding import PartitionSpec as P

HEAD = 64
LEN = 1024
BLK = 128


norm_eps = 1e-05
mask_fill = -1000000000.0


def gelu_exact(value):
    return jax.nn.gelu(value, approximate=False)


def gelu_back(preact, upstream):
    return jax.vjp(gelu_exact, preact)[1](upstream)[0]


def layer_norm(value, gain, bias):
    mean = jnp.mean(value, axis=-1, keepdims=True)
    centred = value - mean
    scale = lax.rsqrt(jnp.mean(centred * centred, axis=-1, keepdims=True) + norm_eps)
    normal = centred * scale
    return (normal * gain + bias, normal, scale)


def norm_back(upstream, normal, scale, gain):
    scaled = upstream * gain
    mean_grad = jnp.mean(scaled, axis=-1, keepdims=True)
    mean_cross = jnp.mean(scaled * normal, axis=-1, keepdims=True)
    inward = scale * (scaled - mean_grad - normal * mean_cross)
    return (inward, jnp.sum(upstream * normal, axis=0), jnp.sum(upstream, axis=0))


def context_allowed(segments, ranks, first, count):
    length = segments.shape[0]
    key_block = jnp.arange(length, dtype=jnp.int32) // BLK
    key_rank = jnp.broadcast_to(ranks[:, None], (ranks.shape[0], BLK)).reshape(length)
    query_segment = lax.dynamic_slice_in_dim(segments, first, count)
    query_rank = lax.dynamic_slice_in_dim(key_rank, first, count)
    query_block = (first + jnp.arange(count, dtype=jnp.int32)) // BLK
    same_doc = query_segment[:, None] == segments[None, :]
    earlier = key_rank[None, :] < query_rank[:, None]
    same_block = query_block[:, None] == key_block[None, :]
    return same_doc & (earlier | same_block)


def full_rows(value):
    return lax.all_gather(value, "tensor", axis=0, tiled=True)


def grad_rows(value):
    return lax.all_gather(value, "tensor", axis=0, tiled=True)


def branch_sum(mixed, weight):
    return lax.psum_scatter(
        jnp.dot(mixed, weight, preferred_element_type=jnp.float32),
        "tensor",
        scatter_dimension=0,
        tiled=True,
    )


def back_product(left, weight):
    return lax.dot_general(
        left, weight, (((1,), (1,)), ((), ())), preferred_element_type=jnp.float32
    )


def row_product(left, right):
    return lax.dot_general(
        left, right, (((0,), (0,)), ((), ())), preferred_element_type=jnp.float32
    )


def input_sum(pairs):
    total = None
    for left, weight in pairs:
        portion = back_product(left, weight)
        total = portion if total is None else total + portion
    return lax.psum_scatter(total, "tensor", scatter_dimension=0, tiled=True)


def split_heads(value, count):
    return value.reshape(count, LEN, value.shape[1] // HEAD, HEAD)


def attend_sequence(query, keys, values, segments, ranks, masked):
    length = query.shape[0]
    width = min(length, 512)

    def one_block(index):
        first = index * width
        piece = lax.dynamic_slice_in_dim(query, first, width, 0)
        scores = jnp.einsum("qhd,khd->hqk", piece, keys, preferred_element_type=jnp.float32) * 0.125
        if masked:
            scores = jnp.where(
                context_allowed(segments, ranks, first, width)[None], scores, mask_fill
            )
        top = jnp.max(scores, axis=-1, keepdims=True)
        raised = jnp.exp(scores - top)
        total = jnp.sum(raised, axis=-1, keepdims=True)
        shares = (raised / total).astype(jnp.bfloat16)
        mixed = jnp.einsum("hqk,khd->qhd", shares, values, preferred_element_type=jnp.float32)
        return (mixed.astype(jnp.bfloat16), (top + jnp.log(total))[..., 0])

    mixed, log_total = lax.map(one_block, jnp.arange(length // width, dtype=jnp.int32))
    return (mixed.reshape(query.shape), log_total)


def attend_sequence_back(query, keys, values, segments, ranks, masked, log_total, grad_mixed):
    length = query.shape[0]
    width = min(length, 512)

    def one_block(carry, index):
        key_sum, value_sum = carry
        first = index * width
        piece = lax.dynamic_slice_in_dim(query, first, width, 0)
        grad_piece = lax.dynamic_slice_in_dim(grad_mixed, first, width, 0)
        scores = jnp.einsum("qhd,khd->hqk", piece, keys, preferred_element_type=jnp.float32) * 0.125
        if masked:
            scores = jnp.where(
                context_allowed(segments, ranks, first, width)[None], scores, mask_fill
            )
        shares = jnp.exp(scores - log_total[index][..., None])
        grad_shares = jnp.einsum(
            "qhd,khd->hqk", grad_piece, values, preferred_element_type=jnp.float32
        )
        inner = jnp.sum(shares * grad_shares, axis=-1, keepdims=True)
        grad_scores = (shares * (grad_shares - inner)).astype(jnp.bfloat16)
        grad_query = (
            jnp.einsum("hqk,khd->qhd", grad_scores, keys, preferred_element_type=jnp.float32)
            * 0.125
        )
        key_sum = (
            key_sum
            + jnp.einsum("hqk,qhd->khd", grad_scores, piece, preferred_element_type=jnp.float32)
            * 0.125
        )
        value_sum = value_sum + jnp.einsum(
            "hqk,qhd->khd",
            shares.astype(jnp.bfloat16),
            grad_piece,
            preferred_element_type=jnp.float32,
        )
        return ((key_sum, value_sum), grad_query.astype(jnp.bfloat16))

    zeros = jnp.zeros(keys.shape, jnp.float32)
    (key_sum, value_sum), grad_query = lax.scan(
        one_block, (zeros, zeros), jnp.arange(length // width, dtype=jnp.int32)
    )
    return (
        grad_query.reshape(query.shape),
        key_sum.astype(jnp.bfloat16),
        value_sum.astype(jnp.bfloat16),
    )


def attend_all(query, keys, values, segments, ranks, masked):
    count = query.shape[0] // LEN

    def one_sequence(items):
        return attend_sequence(items[0], items[1], items[2], items[3], items[4], masked)

    mixed, log_total = lax.map(
        one_sequence,
        (
            split_heads(query, count),
            split_heads(keys, count),
            split_heads(values, count),
            segments,
            ranks,
        ),
    )
    return (mixed.reshape(query.shape), log_total)


def attend_back_all(query, keys, values, segments, ranks, masked, log_total, grad_mixed):
    count = query.shape[0] // LEN

    def one_sequence(items):
        return attend_sequence_back(
            items[0], items[1], items[2], items[3], items[4], masked, items[5], items[6]
        )

    grad_query, grad_keys, grad_values = lax.map(
        one_sequence,
        (
            split_heads(query, count),
            split_heads(keys, count),
            split_heads(values, count),
            segments,
            ranks,
            log_total,
            split_heads(grad_mixed, count),
        ),
    )
    return (
        grad_query.reshape(query.shape),
        grad_keys.reshape(keys.shape),
        grad_values.reshape(values.shape),
    )


def shards(
    tokens,
    encoder_states,
    output_grad,
    valid_mask,
    segment_ids,
    context_ranks,
    self_query,
    self_key,
    self_value,
    self_output,
    cross_query,
    cross_key,
    cross_value,
    cross_output,
    hidden_up,
    hidden_down,
    norm1_gain,
    norm1_bias,
    norm2_gain,
    norm2_bias,
    norm3_gain,
    norm3_bias,
):
    (
        self_query,
        self_key,
        self_value,
        self_output,
        cross_query,
        cross_key,
        cross_value,
        cross_output,
        hidden_up,
        hidden_down,
    ) = (
        lax.all_gather(self_query, "dp", axis=0, tiled=True),
        lax.all_gather(self_key, "dp", axis=0, tiled=True),
        lax.all_gather(self_value, "dp", axis=0, tiled=True),
        lax.all_gather(self_output, "dp", axis=1, tiled=True),
        lax.all_gather(cross_query, "dp", axis=0, tiled=True),
        lax.all_gather(cross_key, "dp", axis=0, tiled=True),
        lax.all_gather(cross_value, "dp", axis=0, tiled=True),
        lax.all_gather(cross_output, "dp", axis=1, tiled=True),
        lax.all_gather(hidden_up, "dp", axis=0, tiled=True),
        lax.all_gather(hidden_down, "dp", axis=1, tiled=True),
    )
    tokens_full = full_rows(tokens)
    query = jnp.dot(tokens_full, self_query, preferred_element_type=jnp.float32).astype(
        jnp.bfloat16
    )
    keys = jnp.dot(tokens_full, self_key, preferred_element_type=jnp.float32).astype(jnp.bfloat16)
    values = jnp.dot(tokens_full, self_value, preferred_element_type=jnp.float32).astype(
        jnp.bfloat16
    )
    self_mixed, self_log = attend_all(query, keys, values, segment_ids, context_ranks, True)
    attended = branch_sum(self_mixed, self_output)
    first_out, first_normal, first_scale = layer_norm(
        tokens.astype(jnp.float32) + attended, norm1_gain, norm1_bias
    )
    first_full = full_rows(first_out.astype(jnp.bfloat16))
    encoder_full = full_rows(encoder_states)
    second_query = jnp.dot(first_full, cross_query, preferred_element_type=jnp.float32).astype(
        jnp.bfloat16
    )
    encoder_keys = jnp.dot(encoder_full, cross_key, preferred_element_type=jnp.float32).astype(
        jnp.bfloat16
    )
    encoder_values = jnp.dot(encoder_full, cross_value, preferred_element_type=jnp.float32).astype(
        jnp.bfloat16
    )
    cross_mixed, cross_log = attend_all(
        second_query, encoder_keys, encoder_values, segment_ids, context_ranks, False
    )
    crossed = branch_sum(cross_mixed, cross_output)
    second_out, second_normal, second_scale = layer_norm(
        first_out + crossed, norm2_gain, norm2_bias
    )
    second_low = second_out.astype(jnp.bfloat16)
    feed_input = full_rows(second_low)
    preact = jnp.dot(feed_input, hidden_up, preferred_element_type=jnp.float32)
    activated = gelu_exact(preact).astype(jnp.bfloat16)
    feed_out = branch_sum(activated, hidden_down)
    third_out, third_normal, third_scale = layer_norm(second_out + feed_out, norm3_gain, norm3_bias)
    valid_rows = valid_mask.astype(jnp.float32)[:, None]
    grad_layer = output_grad.astype(jnp.float32) * valid_rows
    grad_third, gain3_grad, bias3_grad = norm_back(
        grad_layer, third_normal, third_scale, norm3_gain
    )
    grad_third_low = grad_third.astype(jnp.bfloat16)
    grad_feed = grad_rows(grad_third_low)
    grad_active = back_product(grad_feed, hidden_down)
    grad_preact = gelu_back(preact, grad_active).astype(jnp.bfloat16)
    up_grad = row_product(feed_input, grad_preact)
    down_grad = row_product(activated, grad_feed)
    grad_second = grad_third + input_sum([(grad_preact, hidden_up)])
    grad_second_in, gain2_grad, bias2_grad = norm_back(
        grad_second, second_normal, second_scale, norm2_gain
    )
    grad_crossed = grad_rows(grad_second_in.astype(jnp.bfloat16))
    cross_output_grad = row_product(cross_mixed, grad_crossed)
    grad_cross_mixed = back_product(grad_crossed, cross_output).astype(jnp.bfloat16)
    grad_second_query, grad_encoder_keys, grad_encoder_values = attend_back_all(
        second_query,
        encoder_keys,
        encoder_values,
        segment_ids,
        context_ranks,
        False,
        cross_log,
        grad_cross_mixed,
    )
    cross_query_grad = row_product(first_full, grad_second_query)
    cross_key_grad = row_product(encoder_full, grad_encoder_keys)
    cross_value_grad = row_product(encoder_full, grad_encoder_values)
    grad_first = grad_second_in + input_sum([(grad_second_query, cross_query)])
    encoder_grad = input_sum([(grad_encoder_keys, cross_key), (grad_encoder_values, cross_value)])
    grad_first_in, gain1_grad, bias1_grad = norm_back(
        grad_first, first_normal, first_scale, norm1_gain
    )
    grad_attended = grad_rows(grad_first_in.astype(jnp.bfloat16))
    self_output_grad = row_product(self_mixed, grad_attended)
    grad_self_mixed = back_product(grad_attended, self_output).astype(jnp.bfloat16)
    grad_query, grad_keys, grad_values = attend_back_all(
        query, keys, values, segment_ids, context_ranks, True, self_log, grad_self_mixed
    )
    self_query_grad = row_product(tokens_full, grad_query)
    self_key_grad = row_product(tokens_full, grad_keys)
    self_value_grad = row_product(tokens_full, grad_values)
    tokens_grad = grad_first_in + input_sum(
        [(grad_query, self_query), (grad_keys, self_key), (grad_values, self_value)]
    )
    (
        self_query_grad,
        self_key_grad,
        self_value_grad,
        self_output_grad,
        cross_query_grad,
        cross_key_grad,
        cross_value_grad,
        cross_output_grad,
        up_grad,
        down_grad,
    ) = (
        lax.psum_scatter(self_query_grad, "dp", scatter_dimension=0, tiled=True),
        lax.psum_scatter(self_key_grad, "dp", scatter_dimension=0, tiled=True),
        lax.psum_scatter(self_value_grad, "dp", scatter_dimension=0, tiled=True),
        lax.psum_scatter(self_output_grad, "dp", scatter_dimension=1, tiled=True),
        lax.psum_scatter(cross_query_grad, "dp", scatter_dimension=0, tiled=True),
        lax.psum_scatter(cross_key_grad, "dp", scatter_dimension=0, tiled=True),
        lax.psum_scatter(cross_value_grad, "dp", scatter_dimension=0, tiled=True),
        lax.psum_scatter(cross_output_grad, "dp", scatter_dimension=1, tiled=True),
        lax.psum_scatter(up_grad, "dp", scatter_dimension=0, tiled=True),
        lax.psum_scatter(down_grad, "dp", scatter_dimension=1, tiled=True),
    )
    norm_sums, square_sums = lax.psum(
        (
            jnp.stack([gain1_grad, bias1_grad, gain2_grad, bias2_grad, gain3_grad, bias3_grad]),
            jnp.stack(
                [
                    jnp.sum(valid_rows * third_out * third_out, axis=0),
                    jnp.sum(valid_rows * tokens_grad * tokens_grad, axis=0),
                ]
            ),
        ),
        ("dp", "tensor"),
    )
    total_tokens = tokens.shape[0] * lax.axis_size("dp") * lax.axis_size("tensor")
    valid_scales = jnp.sqrt(square_sums / total_tokens)
    return (
        third_out,
        tokens_grad,
        encoder_grad,
        self_query_grad,
        self_key_grad,
        self_value_grad,
        self_output_grad,
        cross_query_grad,
        cross_key_grad,
        cross_value_grad,
        cross_output_grad,
        up_grad,
        down_grad,
        norm_sums,
        valid_scales,
    )


def solution(mesh):
    in_specs = (
        P(("dp", "tensor"), None),
        P(("dp", "tensor"), None),
        P(("dp", "tensor"), None),
        P(("dp", "tensor")),
        P("dp", None),
        P("dp", None),
        P("dp", "tensor"),
        P("dp", "tensor"),
        P("dp", "tensor"),
        P("tensor", "dp"),
        P("dp", "tensor"),
        P("dp", "tensor"),
        P("dp", "tensor"),
        P("tensor", "dp"),
        P("dp", "tensor"),
        P("tensor", "dp"),
        P(),
        P(),
        P(),
        P(),
        P(),
        P(),
    )
    out_specs = (
        P(("dp", "tensor"), None),
        P(("dp", "tensor"), None),
        P(("dp", "tensor"), None),
        P("dp", "tensor"),
        P("dp", "tensor"),
        P("dp", "tensor"),
        P("tensor", "dp"),
        P("dp", "tensor"),
        P("dp", "tensor"),
        P("dp", "tensor"),
        P("tensor", "dp"),
        P("dp", "tensor"),
        P("tensor", "dp"),
        P(),
        P(),
    )
    return jax.shard_map(shards, mesh=mesh, in_specs=in_specs, out_specs=out_specs, check_vma=False)
```

profile of v0, /device:TPU:0, one launch (start us, length us, event | category | flops | bytes accessed | tf_op | source)
XLA Modules:
  0.0 1633.0 jit_solution(10567116157558251906)
XLA Ops:
  8.0 32.6 %all_gather.52 = bf16[512,128]{1,0:T(8,128)(2,1)S(1)} all-gather(bf16[64,128]{1,0:T(8,128)(2,1)} %param.44), channel_id=1, replica_groups=mesh['dp'=8,'tensor'=4] {'dp'}, dimensions={0}, use_global_device_ids=true | all-gather | bytes 147456 | tf_op jit(solution)/shard_map/all_gather | solution.py:246
  40.6 30.8 %all_gather.53 = bf16[512,128]{1,0:T(8,128)(2,1)S(1)} all-gather(bf16[64,128]{1,0:T(8,128)(2,1)} %param.45), channel_id=1, replica_groups=mesh['dp'=8,'tensor'=4] {'dp'}, dimensions={0}, use_global_device_ids=true | all-gather | bytes 147456 | tf_op jit(solution)/shard_map/all_gather | solution.py:247
  102.1 32.7 %all_gather.55 = bf16[128,512]{0,1:T(8,128)(2,1)} all-gather(bf16[128,64]{0,1:T(8,128)(2,1)} %param.47), channel_id=1, replica_groups=mesh['dp'=8,'tensor'=4] {'dp'}, dimensions={1}, use_global_device_ids=true | all-gather | bytes 147456 | tf_op jit(solution)/shard_map/all_gather | solution.py:249
  186.1 44.5 %reduce-scatter.28.cloned.1.call-done = f32[512,512]{1,0:T(8,128)} async-done(((f32[2048,512]{1,0:T(8,128)}), f32[512,512]{1,0:T(8,128)}) %reduce-scatter.28.cloned.1.call-update) | async-done | bytes 1048592 | tf_op jit(solution)/shard_map/reduce_scatter | solution.py:61
  326.3 32.5 %all_gather.61 = bf16[128,512]{0,1:T(8,128)(2,1)} all-gather(bf16[128,64]{0,1:T(8,128)(2,1)S(1)} %copy-done.77), channel_id=1, replica_groups=mesh['dp'=8,'tensor'=4] {'dp'}, dimensions={1}, use_global_device_ids=true | all-gather | bytes 147456 | tf_op jit(solution)/shard_map/all_gather | solution.py:253
  397.9 44.6 %reduce-scatter.30.cloned.1.call-done = f32[512,512]{1,0:T(8,128)} async-done(((f32[2048,512]{1,0:T(8,128)}), f32[512,512]{1,0:T(8,128)}) %reduce-scatter.30.cloned.1.call-update) | async-done | bytes 1048592 | tf_op jit(solution)/shard_map/reduce_scatter | solution.py:61
  445.6 31.4 %all_gather.63 = bf16[512,512]{1,0:T(8,128)(2,1)S(1)} all-gather(bf16[64,512]{1,0:T(8,128)(2,1)S(1)} %copy-done.59), channel_id=1, replica_groups=mesh['dp'=8,'tensor'=4] {'dp'}, dimensions={0}, use_global_device_ids=true | all-gather | bytes 589824 | tf_op jit(solution)/shard_map/all_gather | solution.py:254
  477.0 31.7 %all_gather.64 = bf16[512,512]{0,1:T(8,128)(2,1)S(1)} all-gather(bf16[512,64]{0,1:T(8,128)(2,1)S(1)} %copy-done.60), channel_id=1, replica_groups=mesh['dp'=8,'tensor'=4] {'dp'}, dimensions={1}, use_global_device_ids=true | all-gather | bytes 589824 | tf_op jit(solution)/shard_map/all_gather | solution.py:255
  527.0 44.2 %reduce-scatter.32.cloned.1.call-done = f32[512,512]{1,0:T(8,128)} async-done(((f32[2048,512]{1,0:T(8,128)}), f32[512,512]{1,0:T(8,128)}) %reduce-scatter.32.cloned.1.call-update) | async-done | bytes 1048592 | tf_op jit(solution)/shard_map/reduce_scatter | solution.py:61
  611.9 44.6 %reduce-scatter.34.cloned.1.call-done = f32[512,512]{1,0:T(8,128)} async-done(((f32[2048,512]{1,0:T(8,128)}), f32[512,512]{1,0:T(8,128)}) %reduce-scatter.34.cloned.1.call-update) | async-done | bytes 1048592 | tf_op jit(solution)/shard_map/reduce_scatter | solution.py:86
  691.4 45.9 %while.151 = (s32[]{:T(128)}, bf16[2,1024,2,64]{3,2,1,0:T(2,128)(2,1)}, bf16[2,1024,2,64]{1,3,2,0:T(8,128)(2,1)}, bf16[2,1024,2,64]{1,3,2,0:T(8,128)(2,1)}, bf16...) while((s32[]{:T(128)}, ...), condition=%wide.region_30.31_spmd, body=%wide.region_26.30_spmd.sunk | while | flops 684719104 | bytes 40022608 | solution.py:191
  742.6 44.6 %reduce-scatter.36.cloned.1.call-done = f32[512,512]{1,0:T(8,128)} async-done(((f32[2048,512]{1,0:T(8,128)}), f32[512,512]{1,0:T(8,128)}) %reduce-scatter.36.cloned.1.call-update) | async-done | bytes 1048592 | tf_op jit(solution)/shard_map/reduce_scatter | solution.py:86
  822.1 51.9 %while.153 = (s32[]{:T(128)}, bf16[2,1024,2,64]{3,2,1,0:T(2,128)(2,1)}, bf16[2,1024,2,64]{1,3,2,0:T(8,128)(2,1)}, bf16[2,1024,2,64]{1,3,2,0:T(8,128)(2,1)}, bf16...) while((s32[]{:T(128)}, ...), condition=%wide.region_38.39_spmd, body=%wide.region_34.38_spmd.sunk | while | flops 690502656 | bytes 46359340 | solution.py:191
  932.8 39.9 %all-reduce = (f32[6,512]{1,0:T(8,128)}, f32[2,512]{1,0:T(2,128)S(1)}) all-reduce(f32[6,512]{1,0:T(8,128)S(1)} %stack.36, f32[2,512]{1,0:T(2,128)S(1)} %pad_maximum_fusion), channel_id=1, replica_groups=mesh['dp'=8,'tensor'=4] {'dp','tensor'}, use_global_device_ids=true, to_apply=%region_57.58 | all-reduce | flops 4096 | bytes 32768 | tf_op jit(solution)/shard_map/psum | solution.py:365
  996.8 66.7 %reduce-scatter.50.cloned.1.call-done = f32[512,64]{0,1:T(8,128)} async-done(((f32[512,512]{0,1:T(8,128)}), f32[512,64]{0,1:T(8,128)}) %reduce-scatter.50.cloned.1.call-update) | async-done | bytes 131088 | tf_op jit(solution)/shard_map/reduce_scatter | solution.py:363
  1063.6 64.1 %reduce-scatter.46.cloned.1.call-done = f32[128,64]{0,1:T(8,128)} async-done(((f32[128,512]{0,1:T(8,128)}), f32[128,64]{0,1:T(8,128)}) %reduce-scatter.46.cloned.1.call-update) | async-done | bytes 32784 | tf_op jit(solution)/shard_map/reduce_scatter | solution.py:361
  1127.6 64.1 %reduce-scatter.60.cloned.1.call-done = f32[64,128]{1,0:T(8,128)} async-done(((f32[512,128]{1,0:T(8,128)}), f32[64,128]{1,0:T(8,128)}) %reduce-scatter.60.cloned.1.call-update) | async-done | bytes 32784
  1191.7 64.1 %reduce-scatter.44.cloned.1.call-done = f32[64,128]{1,0:T(8,128)} async-done(((f32[512,128]{1,0:T(8,128)}), f32[64,128]{1,0:T(8,128)}) %reduce-scatter.44.cloned.1.call-update) | async-done | bytes 32784 | tf_op jit(solution)/shard_map/reduce_scatter | solution.py:358
  1255.8 64.2 %reduce-scatter.58.cloned.1.call-done = f32[64,128]{1,0:T(8,128)} async-done(((f32[512,128]{1,0:T(8,128)}), f32[64,128]{1,0:T(8,128)}) %reduce-scatter.58.cloned.1.call-update) | async-done | bytes 32784
  1320.0 46.5 %reduce-scatter.40.cloned.1.call-done = f32[512,512]{1,0:T(8,128)} async-done(((f32[2048,512]{1,0:T(8,128)}), f32[512,512]{1,0:T(8,128)}) %reduce-scatter.40.cloned.1.call-update) | async-done | bytes 1048592 | tf_op jit(solution)/shard_map/reduce_scatter | solution.py:86
  1366.5 65.6 %reduce-scatter.42.cloned.1.call-done = f32[128,64]{0,1:T(8,128)} async-done(((f32[128,512]{0,1:T(8,128)}), f32[128,64]{0,1:T(8,128)}) %reduce-scatter.42.cloned.1.call-update) | async-done | bytes 32784 | tf_op jit(solution)/shard_map/reduce_scatter | solution.py:357
  1432.1 64.6 %reduce-scatter.56.cloned.1.call-done = f32[64,128]{1,0:T(8,128)} async-done(((f32[512,128]{1,0:T(8,128)}), f32[64,128]{1,0:T(8,128)}) %reduce-scatter.56.cloned.1.call-update) | async-done | bytes 32784
  1496.7 64.6 %reduce-scatter.52.cloned.1.call-done = f32[64,128]{1,0:T(8,128)} async-done(((f32[512,128]{1,0:T(8,128)}), f32[64,128]{1,0:T(8,128)}) %reduce-scatter.52.cloned.1.call-update) | async-done | bytes 32784
  1561.3 64.4 %reduce-scatter.54.cloned.1.call-done = f32[64,128]{1,0:T(8,128)} async-done(((f32[512,128]{1,0:T(8,128)}), f32[64,128]{1,0:T(8,128)}) %reduce-scatter.54.cloned.1.call-update) | async-done | bytes 32784
  (608 shorter events, 674.7 us)
Async XLA Ops:
  7.2 127.6 %all-gather.8.cloned.1.call-start = ((), (), s32[]{:S(2)}) async-start(), calls=%async_computation.17 | async-start | bytes 2621440 | tf_op jit(solution)/shard_map/all_gather | solution.py:53
  7.9 222.7 %reduce-scatter.28.cloned.1.call-start = ((), (), s32[]{:S(2)}) async-start(), calls=%async_computation.18 | async-start | bytes 5242880 | tf_op jit(solution)/shard_map/reduce_scatter | solution.py:61
  185.1 173.7 %all-gather.12.cloned.1.call-start = ((), (), s32[]{:S(2)}) async-start(), calls=%async_computation.20 | async-start | bytes 2621440 | tf_op jit(solution)/shard_map/all_gather | solution.py:53
  185.8 182.2 %all-gather.10.cloned.1.call-start = ((), (), s32[]{:S(2)}) async-start(), calls=%async_computation.19 | async-start | bytes 2621440 | tf_op jit(solution)/shard_map/all_gather | solution.py:53
  234.6 208.0 %reduce-scatter.30.cloned.1.call-start = ((), (), s32[]{:S(2)}) async-start(), calls=%async_computation.21 | async-start | bytes 5242880 | tf_op jit(solution)/shard_map/reduce_scatter | solution.py:61
  397.9 110.8 %all-gather.14.cloned.1.call-start = ((), (), s32[]{:S(2)}) async-start(), calls=%async_computation.22 | async-start | bytes 2621440 | tf_op jit(solution)/shard_map/all_gather | solution.py:53
  445.5 125.7 %reduce-scatter.32.cloned.1.call-start = ((), (), s32[]{:S(2)}) async-start(), calls=%async_computation.23 | async-start | bytes 5242880 | tf_op jit(solution)/shard_map/reduce_scatter | solution.py:61
  526.4 74.1 %all-gather.16.cloned.1.call-start = ((), (), s32[]{:S(2)}) async-start(), calls=%async_computation.24 | async-start | bytes 2621440 | tf_op jit(solution)/shard_map/all_gather | solution.py:57
  577.7 78.8 %reduce-scatter.34.cloned.1.call-start = ((), (), s32[]{:S(2)}) async-start(), calls=%async_computation.25 | async-start | bytes 5242880 | tf_op jit(solution)/shard_map/reduce_scatter | solution.py:86
  611.8 71.8 %all-gather.18.cloned.1.call-start = ((), (), s32[]{:S(2)}) async-start(), calls=%async_computation.26 | async-start | bytes 2621440 | tf_op jit(solution)/shard_map/all_gather | solution.py:57
  660.9 126.4 %reduce-scatter.36.cloned.1.call-start = ((), (), s32[]{:S(2)}) async-start(), calls=%async_computation.27 | async-start | bytes 5242880 | tf_op jit(solution)/shard_map/reduce_scatter | solution.py:86
  742.6 71.4 %all-gather.20.cloned.1.call-start = ((), (), s32[]{:S(2)}) async-start(), calls=%async_computation.28 | async-start | bytes 2621440 | tf_op jit(solution)/shard_map/all_gather | solution.py:57
  791.3 138.1 %reduce-scatter.38.cloned.1.call-start = ((), (), s32[]{:S(2)}) async-start(), calls=%async_computation.29 | async-start | bytes 5242880 | tf_op jit(solution)/shard_map/reduce_scatter | solution.py:86
  884.8 112.1 %reduce-scatter.48.cloned.1.call-start = ((), (), s32[]{:S(2)}) async-start(), calls=%async_computation.34 | async-start | bytes 1179648 | tf_op jit(solution)/shard_map/reduce_scatter | solution.py:362
  889.7 173.8 %reduce-scatter.50.cloned.1.call-start = ((), (), s32[]{:S(2)}) async-start(), calls=%async_computation.35 | async-start | bytes 1179648 | tf_op jit(solution)/shard_map/reduce_scatter | solution.py:363
  894.1 233.6 %reduce-scatter.46.cloned.1.call-start = ((), (), s32[]{:S(2)}) async-start(), calls=%async_computation.33 | async-start | bytes 294912 | tf_op jit(solution)/shard_map/reduce_scatter | solution.py:361
  897.6 294.0 %reduce-scatter.60.cloned.1.call-start = ((), (), s32[]{:S(2)}) async-start(), calls=%async_computation.40 | async-start | bytes 294912
  900.7 355.0 %reduce-scatter.44.cloned.1.call-start = ((), (), s32[]{:S(2)}) async-start(), calls=%async_computation.32 | async-start | bytes 294912 | tf_op jit(solution)/shard_map/reduce_scatter | solution.py:358
  903.9 416.1 %reduce-scatter.58.cloned.1.call-start = ((), (), s32[]{:S(2)}) async-start(), calls=%async_computation.39 | async-start | bytes 294912
  908.7 457.8 %reduce-scatter.40.cloned.1.call-start = ((), (), s32[]{:S(2)}) async-start(), calls=%async_computation.30 | async-start | bytes 5242880 | tf_op jit(solution)/shard_map/reduce_scatter | solution.py:86
  912.4 519.7 %reduce-scatter.42.cloned.1.call-start = ((), (), s32[]{:S(2)}) async-start(), calls=%async_computation.31 | async-start | bytes 294912 | tf_op jit(solution)/shard_map/reduce_scatter | solution.py:357
  916.7 580.0 %reduce-scatter.56.cloned.1.call-start = ((), (), s32[]{:S(2)}) async-start(), calls=%async_computation.38 | async-start | bytes 294912
  918.1 643.1 %reduce-scatter.52.cloned.1.call-start = ((), (), s32[]{:S(2)}) async-start(), calls=%async_computation.36 | async-start | bytes 294912
  920.6 705.1 %reduce-scatter.54.cloned.1.call-start = ((), (), s32[]{:S(2)}) async-start(), calls=%async_computation.37 | async-start | bytes 294912
  (97 other events, 2694.9 us)
Sparse Core Ops, SparseCore 0:
  9.6 25.2 all-gather.7
  185.1 45.3 reduce-scatter.27
  232.2 22.5 all-gather.11
  256.9 22.5 all-gather.9
  398.0 44.5 reduce-scatter.29
  445.6 22.5 all-gather.13
  526.5 44.6 reduce-scatter.31
  577.8 22.5 all-gather.15
  611.9 44.5 reduce-scatter.33
  661.0 22.5 all-gather.17
  742.7 44.5 reduce-scatter.35
  791.4 22.5 all-gather.19
  884.9 44.4 reduce-scatter.37
  933.2 63.5 reduce-scatter.47
  1001.0 62.4 reduce-scatter.49
  1067.3 60.2 reduce-scatter.45
  1131.4 60.2 reduce-scatter.59
  1195.4 60.2 reduce-scatter.43
  1259.7 60.2 reduce-scatter.57
  1322.9 43.5 reduce-scatter.39
  1370.8 61.2 reduce-scatter.41
  1436.3 60.2 reduce-scatter.55
  1500.9 60.2 reduce-scatter.51
  1565.4 60.2 reduce-scatter.53
where the time goes:
time: 1640 us; the launch traced here: 1630 us
  waiting for transfers between devices  951 us (58%)
  blocking collectives  354 us (22%)
  matrix products  138 us (8%)
  local copies, waits for them, and re-layouts  91.9 us (6%)
  other arithmetic  53.1 us (3%)
  loops' own time  27.4 us (2%)
    unnamed x29, waiting for transfers between devices  324 us
    reduce_scatter x4, waiting for transfers between devices, input_sum(): return lax.psum_scatter(total, 'tensor', scatter_dimension=0, tiled=True)  142 us
    reduce_scatter x3, waiting for transfers between devices, branch_sum(): lax.psum_scatter(jnp.dot(mixed, weight, preferred_element_type=jnp.float3...  133 us
    all_gather x3, waiting for transfers between devices, grad_rows(): return lax.all_gather(value, 'tensor', axis=0, tiled=True)  67.9 us
    reduce_scatter x1, waiting for transfers between devices, shards(): lax.psum_scatter(down_grad, 'dp', scatter_dimension=1, tiled=True)  66.7 us
    reduce_scatter x1, waiting for transfers between devices, shards(): lax.psum_scatter(self_output_grad, 'dp', scatter_dimension=1, tiled=True)  65.6 us
    reduce_scatter x1, waiting for transfers between devices, shards(): lax.psum_scatter(cross_query_grad, 'dp', scatter_dimension=0, tiled=True)  64.1 us
    reduce_scatter x1, waiting for transfers between devices, shards(): lax.psum_scatter(cross_output_grad, 'dp', scatter_dimension=1, tiled=True)  64.1 us
  transfers between devices with their start and end apart: 24, of which 20 were waited for; matrix products, arithmetic and copies ran while one was open for 3% of the time, Pallas kernels for 0%

commit v1 on v0

--- a/solution.py
+++ b/solution.py
@@ -1,6 +1,8 @@
 import jax
 import jax.numpy as jnp
 from jax import lax
+from jax.experimental import pallas as pl
+from jax.experimental.pallas import tpu as pltpu
 from jax.sharding import PartitionSpec as P
 
 HEAD = 64
@@ -395,6 +397,733 @@
     )
 
 
+MESH = pl.DeviceIdType.MESH
+BF = jnp.bfloat16
+F32 = jnp.float32
+LOG2E = 1.4426950408889634
+SCALE = 0.125 * LOG2E
+CH = 128
+
+
+def nn(a, b):
+    return lax.dot_general(a, b, (((1,), (0,)), ((), ())), preferred_element_type=F32)
+
+
+def nt(a, b):
+    return lax.dot_general(a, b, (((1,), (1,)), ((), ())), preferred_element_type=F32)
+
+
+def turn(x):
+    return x.T
+
+
+class Place:
+    def __init__(self):
+        self.d = lax.axis_index("dp")
+        self.t = lax.axis_index("tensor")
+        self.z, self.y = self.d // 2, self.d % 2
+        self.x, self.c = self.t // 2, self.t % 2
+        self.xt = (1 - self.x) * 2 + self.c
+        self.xn = (self.d, self.xt)
+        self.yn = (self.z * 2 + 1 - self.y, self.t)
+        self.pair = (self.d, self.x * 2 + 1 - self.c)
+        self.zn = [None] + [((((self.z + k) % 4) * 2 + self.y), self.t) for k in (1, 2, 3)]
+
+    def barrier(self):
+        sem = pltpu.get_barrier_semaphore()
+        for dev in [self.xn, self.yn, self.pair] + self.zn[1:]:
+            pl.semaphore_signal(sem, inc=1, device_id=dev, device_id_type=MESH)
+        pl.semaphore_wait(sem, 6)
+
+
+def remote(src, dst, send, recv, dev):
+    return pltpu.make_async_remote_copy(
+        src_ref=src, dst_ref=dst, send_sem=send, recv_sem=recv, device_id=dev, device_id_type=MESH
+    )
+
+
+class Gather:
+    def __init__(self, p, w, cols, ss, rs):
+        self.p, self.w, self.cols, self.ss, self.rs = p, w, cols, ss, rs
+
+    def col(self, t):
+        return pl.ds(pl.multiple_of(t * self.cols, 128), self.cols)
+
+    def blk(self, k, y, t):
+        zs = (self.p.z - k + 4) % 4
+        return self.w.at[:, zs, y, :, self.col(t)]
+
+    def cp(self, ref, i, dev):
+        return remote(ref, ref, self.ss.at[i], self.rs.at[i], dev)
+
+    def own(self):
+        return self.blk(0, self.p.y, self.p.t)
+
+    def z_send(self, k):
+        return self.cp(self.own(), k - 1, self.p.zn[k])
+
+    def z_recv(self, k):
+        return self.cp(self.blk(k, self.p.y, self.p.t), k - 1, self.p.zn[k])
+
+    def x_send(self, k):
+        return self.cp(self.blk(k, self.p.y, self.p.t), 3 + k, self.p.xn)
+
+    def x_recv(self, k):
+        return self.cp(self.blk(k, self.p.y, self.p.xt), 3 + k, self.p.xn)
+
+    def y_send(self, k):
+        return self.cp(self.blk(k, self.p.y, self.p.t), 7 + k, self.p.yn)
+
+    def y_recv(self, k):
+        return self.cp(self.blk(k, 1 - self.p.y, self.p.t), 7 + k, self.p.yn)
+
+    def q_send(self, k):
+        if k < 2:
+            return self.cp(self.blk(k, self.p.y, self.p.xt), 11 + k, self.p.yn)
+        return self.cp(self.blk(k, 1 - self.p.y, self.p.t), 11 + k, self.p.xn)
+
+    def q_recv(self, k):
+        return self.cp(self.blk(k, 1 - self.p.y, self.p.xt), 11 + k, self.p.xn)
+
+    def rail(self, i, core):
+        x = self.p.x if i == 0 else 1 - self.p.x
+        return self.w.at[:, :, :, :, self.col(x * 2 + core)]
+
+    def p_send(self, i):
+        return self.cp(self.rail(i, self.p.c), 15 + i, self.p.pair)
+
+    def p_recv(self, i):
+        return self.cp(self.rail(i, 1 - self.p.c), 15 + i, self.p.pair)
+
+    def start(self):
+        for k in (1, 2, 3):
+            self.z_send(k).start()
+        self.x_send(0).start()
+        self.y_send(0).start()
+
+    def plane(self):
+        for k in (1, 2, 3):
+            self.z_recv(k).wait_recv()
+            self.x_send(k).start()
+            self.y_send(k).start()
+
+    def corner(self):
+        for k in range(4):
+            self.x_recv(k).wait_recv()
+            if k < 2:
+                self.q_send(k).start()
+            self.y_recv(k).wait_recv()
+            if k >= 2:
+                self.q_send(k).start()
+
+    def cross(self):
+        self.p_send(0).start() if False else None
+        for k in range(4):
+            self.q_recv(k).wait_recv()
+        self.p_send(0).start()
+        self.p_send(1).start()
+
+    def finish(self):
+        self.p_recv(0).wait_recv()
+        self.p_recv(1).wait_recv()
+
+    def drain(self):
+        for k in (1, 2, 3):
+            self.z_send(k).wait_send()
+        for k in range(4):
+            self.x_send(k).wait_send()
+            self.y_send(k).wait_send()
+            self.q_send(k).wait_send()
+        self.p_send(0).wait_send()
+        self.p_send(1).wait_send()
+
+
+class Reduce:
+    def __init__(self, p, g, cols, held, r1, r2, r3, out, ss, rs):
+        self.p, self.g, self.cols, self.held = p, g, cols, held
+        self.r1, self.r2, self.r3, self.out, self.ss, self.rs = r1, r2, r3, out, ss, rs
+        self.n = g.shape[0]
+
+    def col(self, t):
+        return pl.ds(pl.multiple_of(t * self.cols, 128), self.cols)
+
+    def cp(self, src, dst, i, dev):
+        return remote(src, dst, self.ss.at[i], self.rs.at[i], dev)
+
+    def pair_copy(self, x):
+        src = self.g.at[:, :, :, :, self.col(x * 2 + 1 - self.p.c)]
+        return self.cp(src, self.held.at[x], x, self.p.pair)
+
+    def corner_copy(self, i):
+        p = self.p
+        src = self.held.at[1 - p.x, :, pl.ds(2 * i, 2), 1 - p.y]
+        return self.cp(src, self.r1.at[i], 2 + i, p.yn if i == 0 else p.xn)
+
+    def plane_copy(self, i):
+        p = self.p
+        src = self.held.at[1 - p.x, :, :, p.y] if i == 0 else self.held.at[p.x, :, :, 1 - p.y]
+        return self.cp(src, self.r2.at[i], 4 + i, p.xn if i == 0 else p.yn)
+
+    def z_copy(self, k):
+        p = self.p
+        src = self.held.at[p.x, :, (p.z + k) % 4, p.y]
+        return self.cp(src, self.r3.at[k - 1], 5 + k, p.zn[k])
+
+    def start(self):
+        self.pair_copy(0).start()
+        self.pair_copy(1).start()
+
+    def corner(self):
+        for x in (0, 1):
+            self.pair_copy(x).wait_recv()
+        for x in (0, 1):
+            col = self.col(x * 2 + self.p.c)
+
+            def one(j, _, x=x, col=col):
+                i, d = j // 8, j % 8
+                mine = self.g[i, d // 2, d % 2, :, col].astype(F32)
+                theirs = self.held[x, i, d // 2, d % 2].astype(F32)
+                self.held[x, i, d // 2, d % 2] = (mine + theirs).astype(BF)
+                return 0
+
+            lax.fori_loop(0, self.n * 8, one, 0)
+        self.corner_copy(0).start()
+        self.corner_copy(1).start()
+
+    def plane(self):
+        p = self.p
+        self.corner_copy(0).wait_recv()
+        self.corner_copy(1).wait_recv()
+        for i in range(self.n):
+            for j in range(2):
+                a = self.held[1 - p.x, i, j, p.y].astype(F32) + self.r1[0, i, j].astype(F32)
+                self.held[1 - p.x, i, j, p.y] = a.astype(BF)
+                b = self.held[p.x, i, 2 + j, 1 - p.y].astype(F32) + self.r1[1, i, j].astype(F32)
+                self.held[p.x, i, 2 + j, 1 - p.y] = b.astype(BF)
+        self.plane_copy(0).start()
+        self.plane_copy(1).start()
+
+    def along(self):
+        p = self.p
+        self.plane_copy(0).wait_recv()
+        self.plane_copy(1).wait_recv()
+        for k in (1, 2, 3):
+            zt = (p.z + k) % 4
+            for i in range(self.n):
+                a = (
+                    self.held[p.x, i, zt, p.y].astype(F32)
+                    + self.r2[0, i, zt].astype(F32)
+                    + self.r2[1, i, zt].astype(F32)
+                )
+                self.held[p.x, i, zt, p.y] = a.astype(BF)
+            self.z_copy(k).start()
+
+    def finish(self):
+        p = self.p
+        for k in (1, 2, 3):
+            self.z_copy(k).wait_recv()
+        for i in range(self.n):
+            a = (
+                self.held[p.x, i, p.z, p.y].astype(F32)
+                + self.r2[0, i, p.z].astype(F32)
+                + self.r2[1, i, p.z].astype(F32)
+            )
+            for k in range(3):
+                a = a + self.r3[k, i].astype(F32)
+            self.out[i] = a
+
+    def drain(self):
+        for i in (0, 1):
+            self.pair_copy(i).wait_send()
+            self.corner_copy(i).wait_send()
+            self.plane_copy(i).wait_send()
+        for k in (1, 2, 3):
+            self.z_copy(k).wait_send()
+
+
+def row_steps(count, one):
+    def body(i, _):
+        one(pl.ds(pl.multiple_of(i * CH, CH), CH))
+        return 0
+
+    lax.fori_loop(0, count // CH, body, 0)
+
+
+def head_half(shape, axis, h):
+    return (lax.broadcasted_iota(jnp.int32, shape, axis) // HEAD) == h
+
+
+def keep_half(value, axis, h):
+    return jnp.where(head_half(value.shape, axis, h), value.astype(F32), 0.0).astype(BF)
+
+
+def attend(qt, k, vt, bias, ot, lse, temp, hooks):
+    def pair(p, _):
+        lanes = pl.ds(pl.multiple_of(p * 128, 128), 128)
+        kp = k[:, lanes]
+        qp = qt[lanes, :]
+        for h in (0, 1):
+            qm = keep_half(qp, 0, h)
+            top = None
+            for i in range(4):
+                rows = slice(i * 256, i * 256 + 256)
+                s = nn(kp[rows], qm) * SCALE
+                if bias is not None:
+                    s = s + bias[rows, :]
+                temp[rows, :] = s
+                m = jnp.max(s, axis=0, keepdims=True)
+                top = m if top is None else jnp.maximum(top, m)
+            total, mixed = None, None
+            vh = vt[pl.ds(pl.multiple_of(p * 128 + h * 64, 64), 64), :]
+            for i in range(4):
+                rows = slice(i * 256, i * 256 + 256)
+                e = jnp.exp2(temp[rows, :] - top)
+                part = jnp.sum(e, axis=0, keepdims=True)
+                total = part if total is None else total + part
+                o = nn(vh[:, rows], e.astype(BF))
+                mixed = o if mixed is None else mixed + o
+            ot[pl.ds(pl.multiple_of(p * 128 + h * 64, 64), 64), :] = mixed * (1.0 / total)
+            lse[pl.ds(p * 2 + h, 1), :] = top + jnp.log2(total)
+        for at, hook in hooks.items():
+            pl.when(p == at)(hook)
+        return 0
+
+    lax.fori_loop(0, 4, pair, 0)
+
+
+def attend_back(q, qt, k, kt, v, do, dot_, ot, bias, lse, dqt, dk_own, dv_own, dkv_send, hooks):
+    def pair(p, _):
+        lanes = pl.ds(pl.multiple_of(p * 128, 128), 128)
+        kp, vp = k[:, lanes], v[:, lanes]
+        qp, dop = qt[lanes, :], dot_[lanes, :]
+        inner = dop.astype(F32) * ot[lanes, :]
+        qms = [keep_half(qp, 0, h) for h in (0, 1)]
+        doms = [keep_half(dop, 0, h) for h in (0, 1)]
+        qr = jnp.concatenate([keep_half(q[:, lanes], 1, h) for h in (0, 1)], axis=0)
+        dor = jnp.concatenate([keep_half(do[:, lanes], 1, h) for h in (0, 1)], axis=0)
+        ds_sum = [jnp.sum(inner[h * 64 : h * 64 + 64], axis=0, keepdims=True) for h in (0, 1)]
+        logs = [lse[pl.ds(p * 2 + h, 1), :] for h in (0, 1)]
+        dq = [None, None]
+        for i in range(4):
+            rows = slice(i * 256, i * 256 + 256)
+            shares, grads = [], []
+            for h in (0, 1):
+                s = nn(kp[rows], qms[h]) * SCALE
+                if bias is not None:
+                    s = s + bias[rows, :]
+                e = jnp.exp2(s - logs[h])
+                dp = nn(vp[rows], doms[h])
+                g = (e * (dp - ds_sum[h])).astype(BF)
+                shares.append(e.astype(BF))
+                grads.append(g)
+                kh = kt[pl.ds(pl.multiple_of(p * 128 + h * 64, 64), 64), rows]
+                part = nn(kh, g)
+                dq[h] = part if dq[h] is None else dq[h] + part
+            dv = nn(jnp.concatenate(shares, axis=1), dor)
+            dk = nn(jnp.concatenate(grads, axis=1), qr) * 0.125
+            if i < 2:
+                dk_own[rows, lanes] = dk
+                dv_own[rows, lanes] = dv
+            else:
+                back = slice(i * 256 - 512, i * 256 - 256)
+                dkv_send[0, back, lanes] = dk.astype(BF)
+                dkv_send[1, back, lanes] = dv.astype(BF)
+        for h in (0, 1):
+            dqt[pl.ds(pl.multiple_of(p * 128 + h * 64, 64), 64), :] = (dq[h] * 0.125).astype(BF)
+        for at, hook in hooks.items():
+            pl.when(p == at)(hook)
+        return 0
+
+    lax.fori_loop(0, 4, pair, 0)
+
+
+def norm_rows(z):
+    mean = jnp.mean(z, axis=-1, keepdims=True)
+    centred = z - mean
+    r = lax.rsqrt(jnp.mean(centred * centred, axis=-1, keepdims=True) + norm_eps)
+    return centred * r, r
+
+
+def norm_back_rows(e, n, r, gain):
+    s = e * gain
+    a = jnp.mean(s, axis=-1, keepdims=True)
+    b = jnp.mean(s * n, axis=-1, keepdims=True)
+    return r * (s - a - n * b)
+
+
+def fast_kernel(
+    x, enc, og, valid, seg, rank,
+    sq, sk, sv, so, cq, ck, cv, co, up, down,
+    g1, b1, g2, b2, g3, b3,
+    y_o, dx_o, eg_o, ga_o, gb_o, gf_o, ns_o, vs_o,
+    wa, wb, wf, ga,
+    q1, qt1, k1, v1, vt1, o1, ot1, l1,
+    q2, qt2, k2, v2, vt2, o2, ot2, l2,
+    bias, n1, n2, r1, r2, h1b, h2b, u, gp, dg, dz, low, lowt, do, dot_,
+    dqt, dq, kvs, kvr1, kvr2, dkv, tt, yb, vcol, st,
+    ha, hb, hf, a1, a2, a3, m1, m2, m3, f1, f2, f3,
+    st_r, gss, grs, rss, rrs, ess, ers, tss, trs, ls,
+):
+    p = Place()
+    p.barrier()
+    G = [
+        Gather(p, w, cols, gss.at[i], grs.at[i])
+        for i, (w, cols) in enumerate(((wa, 128), (wb, 128), (wf, 512)))
+    ]
+    GA, GB, GF = G
+    loads = []
+    for i, (src, w, j, cols) in enumerate(
+        (
+            (sq, wa, 0, 128), (sk, wa, 1, 128), (sv, wa, 2, 128),
+            (ck, wb, 1, 128), (cv, wb, 2, 128), (cq, wb, 3, 128), (up, wf, 0, 512),
+        )
+    ):
+        col = pl.ds(pl.multiple_of(p.t * cols, 128), cols)
+        cp = pltpu.make_async_copy(src, w.at[j, p.z, p.y, :, col], ls.at[i])
+        cp.start()
+        loads.append(cp)
+    for src, w, j, cols in ((so, wb, 0, 128), (co, wb, 4, 128), (down, wf, 1, 512)):
+        col = pl.ds(pl.multiple_of(p.t * cols, 128), cols)
+        w[j, p.z, p.y, :, col] = src[...].astype(F32).T.astype(BF)
+    for cp in loads:
+        cp.wait()
+    GA.start()
+    GB.start()
+    GF.start()
+
+    def mat(w, j):
+        return w[j].reshape(512, w.shape[4])
+
+    st[...] = jnp.zeros_like(st)
+    vcol[...] = jnp.broadcast_to(valid[...].astype(F32), (128, 512)).T
+    own = pl.ds(pl.multiple_of(p.c * 512, 128), 512)
+    other = pl.ds(pl.multiple_of((1 - p.c) * 512, 128), 512)
+    sx = pl.ds(p.x, 1)
+    base = seg[sx, own] * 8
+    high = base + rank[sx, own]
+    for i, half in enumerate((own, other)):
+        code = jnp.broadcast_to(seg[sx, half] * 8 + rank[sx, half], (128, 512)).T
+        for j in range(4):
+            c = code[j * 128 : j * 128 + 128, :1]
+            ok = (c >= base) & (c <= high)
+            bias[i * 512 + j * 128 : i * 512 + j * 128 + 128, :] = jnp.where(ok, 0.0, -2.0e9)
+
+    GA.plane()
+    GA.corner()
+    GA.cross()
+    GB.plane()
+    GA.finish()
+
+    xv = x[...]
+    k1[0:512, :] = nn(xv, mat(wa, 1)).astype(BF)
+    v1[0:512, :] = nn(xv, mat(wa, 2)).astype(BF)
+
+    def swap(buf, i):
+        return remote(buf.at[pl.ds(0, 512)], buf.at[pl.ds(512, 512)], ess.at[i], ers.at[i], p.pair)
+
+    swap(k1, 0).start()
+    swap(v1, 1).start()
+    qv = nn(xv, mat(wa, 0)).astype(BF)
+    q1[...] = qv
+    qt1[...] = turn(qv)
+    GB.corner()
+    GF.plane()
+    swap(k1, 0).wait_recv()
+    swap(v1, 1).wait_recv()
+    vt1[...] = turn(v1[...])
+    attend(qt1, k1, vt1, bias, ot1, l1, gp, {0: GB.cross, 2: GF.corner})
+    o1[...] = turn(ot1[...].astype(BF))
+    GB.finish()
+    ev = enc[...]
+    k2[0:512, :] = nn(ev, mat(wb, 1)).astype(BF)
+    v2[0:512, :] = nn(ev, mat(wb, 2)).astype(BF)
+    swap(k2, 2).start()
+    swap(v2, 3).start()
+    yb[...] = nt(o1[...], mat(wb, 0))
+
+    def first(r):
+        n, s = norm_rows(x[r, :].astype(F32) + yb[r, :])
+        n1[r, :] = n
+        r1[r, :] = s
+        h1b[r, :] = (n * g1[...] + b1[...]).astype(BF)
+
+    row_steps(512, first)
+    qv = nn(h1b[...], mat(wb, 3)).astype(BF)
+    q2[...] = qv
+    qt2[...] = turn(qv)
+    swap(k2, 2).wait_recv()
+    swap(v2, 3).wait_recv()
+    vt2[...] = turn(v2[...])
+    attend(qt2, k2, vt2, None, ot2, l2, gp, {0: GF.cross})
+    o2[...] = turn(ot2[...].astype(BF))
+    yb[...] = nt(o2[...], mat(wb, 4))
+
+    def second(r):
+        n, s = norm_rows(n1[r, :] * g1[...] + b1[...] + yb[r, :])
+        n2[r, :] = n
+        r2[r, :] = s
+        h2b[r, :] = (n * g2[...] + b2[...]).astype(BF)
+
+    row_steps(512, second)
+    GF.finish()
+    hv = h2b[...]
+    for j in range(4):
+        cols = slice(j * 512, j * 512 + 512)
+        gp[cols, :] = nn(hv, wf[0, :, :, :, cols].reshape(512, 512))
+
+        def gelu(r, j=j, cols=cols):
+            at = pl.ds(pl.multiple_of(r.start + j * 512, CH), CH)
+            v = gp[at, :]
+            cdf = 0.5 * (1.0 + lax.erf(v * 0.7071067811865476))
+            u[r, cols] = (v * cdf).astype(BF)
+            gp[at, :] = cdf + v * (jnp.exp2(v * v * (-0.5 * LOG2E)) * 0.3989422804014327)
+
+        row_steps(512, gelu)
+    yb[...] = nt(u[...], mat(wf, 1))
+
+    def third(r):
+        n, s = norm_rows(n2[r, :] * g2[...] + b2[...] + yb[r, :])
+        out = n * g3[...] + b3[...]
+        vc = vcol[r, :1]
+        yb[r, :] = out
+        e = og[r, :].astype(F32) * vc
+        st[4:5, :] += jnp.sum(e * n, axis=0, keepdims=True)
+        st[5:6, :] += jnp.sum(e, axis=0, keepdims=True)
+        st[6:7, :] += jnp.sum(vc * out * out, axis=0, keepdims=True)
+        back = norm_back_rows(e, n, s, g3[...])
+        dz[r, :] = back
+        low[r, :] = back.astype(BF)
+
+    row_steps(512, third)
+    y_copy = pltpu.make_async_copy(yb, y_o, ls.at[7])
+    y_copy.start()
+    lv = low[...]
+    lowt[...] = turn(lv)
+    for j in range(4):
+        cols = slice(j * 512, j * 512 + 512)
+        dg[:, cols] = (nn(lv, wf[1, :, :, :, cols].reshape(512, 512)) * gp[cols, :]).astype(BF)
+    dz[...] += nt(dg[...], mat(wf, 0))
+    for g in G:
+        g.drain()
+    tt[...] = turn(h2b[...])
+    for j in range(4):
+        cols = slice(j * 512, j * 512 + 512)
+        wf[0, :, :, :, cols] = nn(tt[...], dg[:, cols]).astype(BF).reshape(4, 2, 64, 512)
+        wf[1, :, :, :, cols] = nn(lowt[...], u[:, cols]).astype(BF).reshape(4, 2, 64, 512)
+    R = [
+        Reduce(p, *args, rss.at[i], rrs.at[i])
+        for i, args in enumerate(
+            (
+                (ga, 128, ha, a1, a2, a3, ga_o),
+                (wb, 128, hb, m1, m2, m3, gb_o),
+                (wf, 512, hf, f1, f2, f3, gf_o),
+            )
+        )
+    ]
+    RA, RB, RF = R
+    RF.start()
+
+    def back2(r):
+        e = dz[r, :]
+        n = n2[r, :]
+        st[2:3, :] += jnp.sum(e * n, axis=0, keepdims=True)
+        st[3:4, :] += jnp.sum(e, axis=0, keepdims=True)
+        back = norm_back_rows(e, n, r2[r, :], g2[...])
+        dz[r, :] = back
+        low[r, :] = back.astype(BF)
+
+    row_steps(512, back2)
+    dov = nn(low[...], mat(wb, 4)).astype(BF)
+    do[...] = dov
+    dot_[...] = turn(dov)
+    lowt[...] = turn(low[...])
+    wb[4] = nn(lowt[...], o2[...]).astype(BF).reshape(4, 2, 64, 512)
+    vt2[...] = turn(k2[...])
+    attend_back(
+        q2, qt2, k2, vt2, v2, do, dot_, ot2, None, l2, dqt,
+        gp.at[pl.ds(0, 512)], gp.at[pl.ds(512, 512)], kvs,
+        {0: RF.corner, 1: RF.plane, 3: RF.along},
+    )
+
+    def swap_back(buf, i):
+        return remote(kvs, buf, ess.at[i], ers.at[i], p.pair)
+
+    swap_back(kvr2, 4).start()
+    dqv = turn(dqt[...])
+    dz[...] += nt(dqv, mat(wb, 3))
+    tt[...] = turn(h1b[...])
+    wb[3] = nn(tt[...], dqv).astype(BF).reshape(4, 2, 64, 512)
+
+    def back1(r):
+        e = dz[r, :]
+        n = n1[r, :]
+        st[0:1, :] += jnp.sum(e * n, axis=0, keepdims=True)
+        st[1:2, :] += jnp.sum(e, axis=0, keepdims=True)
+        back = norm_back_rows(e, n, r1[r, :], g1[...])
+        dz[r, :] = back
+        low[r, :] = back.astype(BF)
+
+    row_steps(512, back1)
+    dov = nn(low[...], mat(wb, 0)).astype(BF)
+    do[...] = dov
+    dot_[...] = turn(dov)
+    lowt[...] = turn(low[...])
+    wb[0] = nn(lowt[...], o1[...]).astype(BF).reshape(4, 2, 64, 512)
+    vt1[...] = turn(k1[...])
+    swap_back(kvr2, 4).wait()
+
+    def join(recv, at):
+        def one(r):
+            for i in (0, 1):
+                own_rows = pl.ds(pl.multiple_of(r.start + at + i * 512, CH), CH)
+                dkv[i, r, :] = (gp[own_rows, :] + recv[i, r, :].astype(F32)).astype(BF)
+
+        row_steps(512, one)
+
+    join(kvr2, 0)
+    y_copy.wait()
+    yb[...] = nt(dkv[0], mat(wb, 1)) + nt(dkv[1], mat(wb, 2))
+    e_copy = pltpu.make_async_copy(yb, eg_o, ls.at[7])
+    e_copy.start()
+    tt[...] = turn(enc[...])
+    wb[1] = nn(tt[...], dkv[0]).astype(BF).reshape(4, 2, 64, 512)
+    wb[2] = nn(tt[...], dkv[1]).astype(BF).reshape(4, 2, 64, 512)
+    RB.start()
+    attend_back(
+        q1, qt1, k1, vt1, v1, do, dot_, ot1, bias, l1, dqt,
+        gp.at[pl.ds(1024, 512)], gp.at[pl.ds(1536, 512)], kvs,
+        {0: RB.corner, 1: RB.plane, 2: RF.finish, 3: RB.along},
+    )
+    swap_back(kvr1, 5).start()
+    tt[...] = turn(x[...])
+    dqv = turn(dqt[...])
+    ga[0] = nn(tt[...], dqv).astype(BF).reshape(4, 2, 64, 512)
+    dz[...] += nt(dqv, mat(wa, 0))
+    swap_back(kvr1, 5).wait()
+    join(kvr1, 1024)
+    ga[1] = nn(tt[...], dkv[0]).astype(BF).reshape(4, 2, 64, 512)
+    ga[2] = nn(tt[...], dkv[1]).astype(BF).reshape(4, 2, 64, 512)
+    RA.start()
+    dz[...] += nt(dkv[0], mat(wa, 1)) + nt(dkv[1], mat(wa, 2))
+    RA.corner()
+    x_copy = pltpu.make_async_copy(dz, dx_o, ls.at[8])
+    x_copy.start()
+
+    def squares(r):
+        st[7:8, :] += jnp.sum(vcol[r, :1] * dz[r, :] * dz[r, :], axis=0, keepdims=True)
+
+    row_steps(512, squares)
+
+    def stat(i, src, dev):
+        return remote(src, st_r.at[i], tss.at[i], trs.at[i], dev)
+
+    stat(0, st, p.pair).start()
+    RA.plane()
+    RB.finish()
+    stat(0, st, p.pair).wait()
+    st_r[6] = st[...] + st_r[0]
+    stat(1, st_r.at[6], p.xn).start()
+    stat(1, st_r.at[6], p.xn).wait()
+    st_r[7] = st_r[6] + st_r[1]
+    stat(2, st_r.at[7], p.yn).start()
+    RA.along()
+    stat(2, st_r.at[7], p.yn).wait()
+    st_r[8] = st_r[7] + st_r[2]
+    for k in (1, 2, 3):
+        stat(2 + k, st_r.at[8], p.zn[k]).start()
+    RA.finish()
+    for k in (1, 2, 3):
+        stat(2 + k, st_r.at[8], p.zn[k]).wait()
+    total = None
+    for zs in range(4):
+        part = None
+        for k in range(4):
+            got = st_r[8] if k == 0 else st_r[2 + k]
+            got = jnp.where((p.z - k + 4) % 4 == zs, got, 0.0)
+            part = got if part is None else part + got
+        total = part if total is None else total + part
+    ns_o[...] = total[0:6]
+    vs_o[...] = jnp.sqrt(total[6:8] * (1.0 / 16384.0))
+    for i in range(4):
+        swap((k1, v1, k2, v2)[i], i).wait_send()
+    for r in R:
+        r.drain()
+    e_copy.wait()
+    x_copy.wait()
+
+
+def fast_shards(
+    tokens, encoder_states, output_grad, valid_mask, segment_ids, context_ranks,
+    self_query, self_key, self_value, self_output,
+    cross_query, cross_key, cross_value, cross_output, hidden_up, hidden_down,
+    norm1_gain, norm1_bias, norm2_gain, norm2_bias, norm3_gain, norm3_bias,
+):
+    vm = pl.BlockSpec(memory_space=pltpu.VMEM)
+    hbm = pl.BlockSpec(memory_space=pl.ANY)
+    ranks = jnp.repeat(context_ranks, BLK, axis=1)
+    rows = [
+        v.reshape(1, 512)
+        for v in (norm1_gain, norm1_bias, norm2_gain, norm2_bias, norm3_gain, norm3_bias)
+    ]
+
+    def V(*shape, dtype=BF):
+        return pltpu.VMEM(shape, dtype)
+
+    def S(*shape):
+        return pltpu.SemaphoreType.DMA(shape)
+
+    def group(n, cols):
+        return [
+            V(2, n, 4, 2, 64, cols),
+            [V(2, n, 2, 64, cols), V(2, n, 4, 64, cols), V(3, n, 64, cols)],
+        ]
+
+    ra, rb, rf = group(3, 128), group(5, 128), group(2, 512)
+
+    def attention():
+        return [
+            V(512, 512), V(512, 512), V(1024, 512), V(1024, 512), V(512, 1024), V(512, 512),
+            V(512, 512, dtype=F32), V(8, 512, dtype=F32),
+        ]
+
+    scratch = (
+        [V(3, 4, 2, 64, 512), V(5, 4, 2, 64, 512), V(2, 4, 2, 64, 2048), V(3, 4, 2, 64, 512)]
+        + attention()
+        + attention()
+        + [V(1024, 512, dtype=F32), V(512, 512, dtype=F32), V(512, 512, dtype=F32)]
+        + [V(512, 1, dtype=F32), V(512, 1, dtype=F32), V(512, 512), V(512, 512)]
+        + [V(512, 2048), V(2048, 512, dtype=F32), V(512, 2048), V(512, 512, dtype=F32)]
+        + [V(512, 512)] * 4
+        + [V(512, 512), V(512, 512), V(2, 512, 512), V(2, 512, 512), V(2, 512, 512), V(2, 512, 512)]
+        + [V(512, 512), V(512, 512, dtype=F32), V(512, 128, dtype=F32), V(8, 512, dtype=F32)]
+        + [ra[0], rb[0], rf[0]]
+        + ra[1] + rb[1] + rf[1]
+        + [V(9, 8, 512, dtype=F32)]
+        + [S(3, 17), S(3, 17), S(3, 9), S(3, 9), S(6), S(6), S(6), S(6), S(9)]
+    )
+    big = jax.ShapeDtypeStruct((512, 512), F32)
+    outs = pl.pallas_call(
+        fast_kernel,
+        out_shape=[big, big, big]
+        + [jax.ShapeDtypeStruct(s, F32) for s in ((3, 64, 128), (5, 64, 128), (2, 64, 512), (6, 512), (2, 512))],
+        in_specs=[vm] * 6 + [hbm] * 3 + [vm] + [hbm] * 3 + [vm] + [hbm] + [vm] + [vm] * 6,
+        out_specs=[hbm] * 3 + [vm] * 5,
+        scratch_shapes=scratch,
+        compiler_params=pltpu.CompilerParams(
+            collective_id=0, has_side_effects=True, vmem_limit_bytes=60 << 20
+        ),
+        name="layer",
+    )(
+        tokens, encoder_states, output_grad, valid_mask.reshape(1, 512), segment_ids, ranks,
+        self_query, self_key, self_value, self_output,
+        cross_query, cross_key, cross_value, cross_output, hidden_up, hidden_down, *rows,
+    )
+    y, dx, eg, ga, gb, gf, ns, vs = outs
+    return (
+        y, dx, eg, ga[0], ga[1], ga[2], gb[0].T, gb[3], gb[1], gb[2], gb[4].T, gf[0], gf[1].T, ns, vs,
+    )
+
+
 def solution(mesh):
     in_specs = (
         P(("dp", "tensor"), None),
@@ -437,4 +1166,5 @@
         P(),
         P(),
     )
-    return jax.shard_map(shards, mesh=mesh, in_specs=in_specs, out_specs=out_specs, check_vma=False)
+    body = fast_shards if dict(mesh.shape) == {"dp": 8, "tensor": 4} else shards
+    return jax.shard_map(body, mesh=mesh, in_specs=in_specs, out_specs=out_specs, check_vma=False)

time: 1640 us -> 160 us (0.10)
  waiting for transfers between devices: 951 us -> 0 us
  blocking collectives: 354 us -> 0 us
  Pallas kernels: 0 us -> 146 us
  matrix products: 138 us -> 0 us
  local copies, waits for them, and re-layouts: 91.9 us -> 12.3 us
  other arithmetic: 53.1 us -> 0 us
  loops' own time: 27.4 us -> 0 us
    reduce_scatter x12 -> x0, waiting for transfers between devices: 559 us -> none  [the longest x4 142 us: input_sum(): return lax.psum_scatter(total, 'tensor', scatter_dimension=0, tiled=True)]
    unnamed x29 -> x0, waiting for transfers between devices: 324 us -> none
    all_gather x10 -> x0, blocking collectives: 314 us -> none  [the longest x1 32.7 us: shards(): lax.all_gather(self_output, 'dp', axis=1, tiled=True)]
    pallas_call x0 -> x1, Pallas kernels: none -> 146 us  [fast_shards(): pl.pallas_call(fast_kernel, out_shape=[big, big, big] + [jax.ShapeDtypeSt...]
    dot_general x86 -> x0, matrix products: 138 us -> none  [the longest x10 25.2 us: back_product(): lax.dot_general(left, weight, (((1,), (1,)), ((), ())), preferred_element...]
    all_gather x7 -> x0, waiting for transfers between devices: 67.9 us -> none  [the longest x3 67.9 us: grad_rows(): return lax.all_gather(value, 'tensor', axis=0, tiled=True)]
    psum x1 -> x0, blocking collectives: 39.9 us -> none  [shards(): lax.psum((jnp.stack([gain1_grad, bias1_grad, gain2_grad, bias2_grad, gain...]
    another operation x12 -> x0, loops' own time: 27.4 us -> none  [the longest x4 21.4 us: attend_sequence_back(): lax.scan(one_block, (zeros, zeros), jnp.arange(length // width, dtype=jnp...]
  transfers between devices with their start and end apart: 24 -> 0, of which waited for: 20 -> 0; matrix products, arithmetic and copies ran while one was open for 3% -> 0% of each run, Pallas kernels for 0% -> 0%
where the time goes in v1:
time: 160 us; the launch traced here: 159 us
  Pallas kernels  146 us (91%)
  local copies, waits for them, and re-layouts  12.3 us (8%)
    pallas_call x1, Pallas kernels, fast_shards(): pl.pallas_call(fast_kernel, out_shape=[big, big, big] + [jax.ShapeDtypeSt...  146 us
    unnamed x28, local copies, waits for them, and re-layouts  8.99 us

profile of v1, /device:TPU:0, one launch (start us, length us, event | category | flops | bytes accessed | tf_op | source)
XLA Modules:
  0.0 159.3 jit_solution(16687775130884675396)
XLA Ops:
  0.6 0.0 copy-start
  0.7 0.0 copy-start.5
  0.7 0.0 copy-start.6
  0.7 0.0 copy-start.4
  0.7 0.6 copy-done
  1.3 0.1 broadcast_bitcast_fusion
  1.4 0.6 copy.42
  2.0 0.0 copy-done.5
  2.0 0.7 copy.37.so
  2.7 0.0 copy-done.6
  2.7 0.7 copy.38.co
  3.5 0.8 copy.39.down
  4.2 146.3 %layer.1 = (f32[512,512]{1,0:T(8,128)}, f32[512,512]{1,0:T(8,128)}, f32[512,512]{1,0:T(8,128)}, f32[3,64,128]{2,1,0:T(8,128)}, f32[5,64,128]{2,1,0:T(8,128)}, /*...) custom-call(bf16[512,512]{1,0:T(8,128)(2,1)} %x.1, bf16[512,512]{1,0:T(8,128)(2,1)} %enc.1, ...), custom_call_target="tpu_custom_call" | custom-call | tf_op jit(solution)/shard_map/layer/pallas_call | solution.py:1105
  150.5 1.7 %slice_bitcast_fusion.2 = (f32[128,64]{0,1:T(8,128)}, f32[64,128]{1,0:T(8,128)}, f32[64,128]{1,0:T(8,128)}, f32[64,128]{1,0:T(8,128)}, f32[128,64]{0,1:T(8,128)}...) fusion(f32[5,64,128]{2,1,0:T(8,128)} %get-tuple-element.27, f32[3,64,128]{2,1,0:T(8,128)} %get-tuple-element.26), kind=kLoop, calls=%fused_computation.2 | loop fusion | bytes 524288 | tf_op jit(solution)/shard_map/transpose | solution.py:1123
  152.1 1.7 %slice_bitcast_fusion = (f32[512,64]{0,1:T(8,128)}, f32[64,512]{1,0:T(8,128)}) fusion(f32[2,64,512]{2,1,0:T(8,128)} %get-tuple-element.28), kind=kLoop, calls=%fused_computation | loop fusion | bytes 524288 | tf_op jit(solution)/shard_map/transpose | solution.py:1123
  153.8 1.0 copy.48
  154.8 0.6 copy-done.2
  155.4 1.0 copy.49
  156.4 0.6 copy-done.1
  157.0 1.0 copy.50
  158.0 0.0 copy-done.7
  158.0 0.6 copy.51
  158.6 0.1 copy-done.8
  158.7 0.6 copy.52
  (7 shorter events, 0.0 us)
Async XLA Ops:
  0.6 0.7 copy-start
  0.7 1.4 copy-start.5
  0.7 2.1 %copy-start.6 = (bf16[128,64]{0,1:T(8,128)(2,1)S(1)}, bf16[128,64]{0,1:T(8,128)(2,1)}, u32[]{:S(2)}) copy-start(bf16[128,64]{0,1:T(8,128)(2,1)} %param.35) | copy-start | bytes 49156
  0.7 2.8 %copy-start.4 = (bf16[512,64]{0,1:T(8,128)(2,1)S(1)}, bf16[512,64]{0,1:T(8,128)(2,1)}, u32[]{:S(2)}) copy-start(bf16[512,64]{0,1:T(8,128)(2,1)} %param.37) | copy-start | bytes 196612
  150.5 3.4 %copy-start.3 = (f32[512,512]{1,0:T(8,128)S(1)}, f32[512,512]{1,0:T(8,128)}, u32[]{:S(2)}) copy-start(f32[512,512]{1,0:T(8,128)} %get-tuple-element.59) | copy-start | bytes 3145732
  153.8 1.6 %copy-start.2 = (f32[512,512]{1,0:T(8,128)S(1)}, f32[512,512]{1,0:T(8,128)}, u32[]{:S(2)}) copy-start(f32[512,512]{1,0:T(8,128)} %get-tuple-element.60) | copy-start | bytes 3145732
  155.4 1.6 %copy-start.1 = (f32[512,512]{1,0:T(8,128)S(1)}, f32[512,512]{1,0:T(8,128)}, u32[]{:S(2)}) copy-start(f32[512,512]{1,0:T(8,128)} %get-tuple-element.61) | copy-start | bytes 3145732
  157.0 1.0 copy-start.7
  158.0 0.7 copy-start.8

commit v2 on v1

--- a/solution.py
+++ b/solution.py
@@ -495,15 +495,20 @@
     def p_recv(self, i):
         return self.cp(self.rail(i, 1 - self.p.c), 15 + i, self.p.pair)
 
-    def start(self):
+    def zs(self):
         for k in (1, 2, 3):
             self.z_send(k).start()
+
+    def oxy(self):
         self.x_send(0).start()
         self.y_send(0).start()
 
-    def plane(self):
+    def plane(self, *between):
         for k in (1, 2, 3):
             self.z_recv(k).wait_recv()
+            if k == 1:
+                for fn in between:
+                    fn()
             self.x_send(k).start()
             self.y_send(k).start()
 
@@ -515,12 +520,11 @@
             self.y_recv(k).wait_recv()
             if k >= 2:
                 self.q_send(k).start()
+        self.p_send(0).start()
 
     def cross(self):
-        self.p_send(0).start() if False else None
         for k in range(4):
             self.q_recv(k).wait_recv()
-        self.p_send(0).start()
         self.p_send(1).start()
 
     def finish(self):
@@ -641,6 +645,97 @@
             self.z_copy(k).wait_send()
 
 
+class Tail:
+    def __init__(self, p, gt, hp, hx, hy, hz, out, ss, rs):
+        self.p, self.gt, self.hp, self.hx, self.hy, self.hz = p, gt, hp, hx, hy, hz
+        self.out, self.ss, self.rs = out, ss, rs
+
+    def cp(self, src, dst, i, dev):
+        return remote(src, dst, self.ss.at[i], self.rs.at[i], dev)
+
+    def pair_copy(self, j):
+        return self.cp(self.gt.at[j], self.hp.at[j // 2], j, self.p.pair)
+
+    def x_copy(self, j):
+        return self.cp(self.gt.at[j], self.hx, 4, self.p.xn)
+
+    def y_copy(self, j):
+        return self.cp(self.gt.at[j, :, :, 1 - self.p.y], self.hy, 5, self.p.yn)
+
+    def z_copy(self, j, k):
+        p = self.p
+        return self.cp(self.gt.at[j, :, (p.z + k) % 4, p.y], self.hz.at[k - 1], 5 + k, p.zn[k])
+
+    def mine(self, j, fn):
+        pl.when(self.p.c == j % 2)(fn)
+
+    def start(self, j):
+        pl.when(self.p.c != j % 2)(lambda: self.pair_copy(j).start())
+
+    def sum_pair(self, j):
+        def do():
+            self.pair_copy(j).wait_recv()
+            if j >= 2:
+                self.x_copy(j).wait_recv()
+
+            def one(i, _):
+                w, d = i // 8, i % 8
+                at = (w, d // 2, d % 2)
+                a = self.gt[(j,) + at].astype(F32) + self.hp[(j // 2,) + at].astype(F32)
+                if j >= 2:
+                    a = a + self.hx[at].astype(F32)
+                self.gt[(j,) + at] = a.astype(BF)
+                return 0
+
+            lax.fori_loop(0, 24, one, 0)
+            if j < 2:
+                self.x_copy(j).start()
+            else:
+                self.y_copy(j).start()
+
+        self.mine(j, do)
+
+    def sum_y(self, j):
+        def do():
+            p = self.p
+            self.y_copy(j).wait_recv()
+            for i in range(3):
+                for k in (1, 2, 3):
+                    zt = (p.z + k) % 4
+                    a = self.gt[j, i, zt, p.y].astype(F32) + self.hy[i, zt].astype(F32)
+                    self.gt[j, i, zt, p.y] = a.astype(BF)
+            for k in (1, 2, 3):
+                self.z_copy(j, k).start()
+
+        self.mine(j, do)
+
+    def finish(self, j):
+        def do():
+            p = self.p
+            for k in (1, 2, 3):
+                self.z_copy(j, k).wait_recv()
+            for i in range(3):
+                a = self.gt[j, i, p.z, p.y].astype(F32) + self.hy[i, p.z].astype(F32)
+                for k in range(3):
+                    a = a + self.hz[k, i].astype(F32)
+                self.out[i] = a
+
+        self.mine(j, do)
+
+    def drain(self):
+        for j in range(4):
+            pl.when(self.p.c != j % 2)(lambda j=j: self.pair_copy(j).wait_send())
+
+        def sent(j):
+            self.x_copy(j).wait_send()
+            self.y_copy(j + 2).wait_send()
+            for k in (1, 2, 3):
+                self.z_copy(j + 2, k).wait_send()
+
+        for j in (0, 1):
+            self.mine(j, lambda j=j: sent(j))
+
+
 def row_steps(count, one):
     def body(i, _):
         one(pl.ds(pl.multiple_of(i * CH, CH), CH))
@@ -655,6 +750,12 @@
 
 def keep_half(value, axis, h):
     return jnp.where(head_half(value.shape, axis, h), value.astype(F32), 0.0).astype(BF)
+
+
+def run_hooks(hooks, step, half):
+    for (at, part), hook in hooks.items():
+        if part == half:
+            pl.when(step == at)(hook)
 
 
 def attend(qt, k, vt, bias, ot, lse, temp, hooks):
@@ -684,15 +785,15 @@
                 mixed = o if mixed is None else mixed + o
             ot[pl.ds(pl.multiple_of(p * 128 + h * 64, 64), 64), :] = mixed * (1.0 / total)
             lse[pl.ds(p * 2 + h, 1), :] = top + jnp.log2(total)
-        for at, hook in hooks.items():
-            pl.when(p == at)(hook)
+            run_hooks(hooks, p, h)
         return 0
 
     lax.fori_loop(0, 4, pair, 0)
 
 
-def attend_back(q, qt, k, kt, v, do, dot_, ot, bias, lse, dqt, dk_own, dv_own, dkv_send, hooks):
-    def pair(p, _):
+def attend_back(q, qt, k, kt, v, do, dot_, ot, bias, lse, dqt, dk_own, dv_own, dkv_send, order, hooks):
+    def pair(step, _):
+        p = order(step)
         lanes = pl.ds(pl.multiple_of(p * 128, 128), 128)
         kp, vp = k[:, lanes], v[:, lanes]
         qp, dop = qt[lanes, :], dot_[lanes, :]
@@ -728,10 +829,11 @@
                 back = slice(i * 256 - 512, i * 256 - 256)
                 dkv_send[0, back, lanes] = dk.astype(BF)
                 dkv_send[1, back, lanes] = dv.astype(BF)
+            if i == 1:
+                run_hooks(hooks, step, 0)
         for h in (0, 1):
             dqt[pl.ds(pl.multiple_of(p * 128 + h * 64, 64), 64), :] = (dq[h] * 0.125).astype(BF)
-        for at, hook in hooks.items():
-            pl.when(p == at)(hook)
+        run_hooks(hooks, step, 1)
         return 0
 
     lax.fori_loop(0, 4, pair, 0)
@@ -752,44 +854,47 @@
 
 
 def fast_kernel(
-    x, enc, og, valid, seg, rank,
+    x_i, enc_i, og_i, valid, seg, rank,
     sq, sk, sv, so, cq, ck, cv, co, up, down,
     g1, b1, g2, b2, g3, b3,
     y_o, dx_o, eg_o, ga_o, gb_o, gf_o, ns_o, vs_o,
-    wa, wb, wf, ga,
+    x, enc, og, codes, wa, wb, wf, gt,
     q1, qt1, k1, v1, vt1, o1, ot1, l1,
     q2, qt2, k2, v2, vt2, o2, ot2, l2,
     bias, n1, n2, r1, r2, h1b, h2b, u, gp, dg, dz, low, lowt, do, dot_,
     dqt, dq, kvs, kvr1, kvr2, dkv, tt, yb, vcol, st,
-    ha, hb, hf, a1, a2, a3, m1, m2, m3, f1, f2, f3,
-    st_r, gss, grs, rss, rrs, ess, ers, tss, trs, ls,
+    hb, hu, hd, m1, m2, m3, u1, u2, u3, d1, d2, d3, hp, hx, hy, hz,
+    st_r, gss, grs, rss, rrs, aas, ars, ess, ers, tss, trs, ls,
 ):
     p = Place()
-    p.barrier()
-    G = [
-        Gather(p, w, cols, gss.at[i], grs.at[i])
-        for i, (w, cols) in enumerate(((wa, 128), (wb, 128), (wf, 512)))
-    ]
-    GA, GB, GF = G
     loads = []
     for i, (src, w, j, cols) in enumerate(
         (
             (sq, wa, 0, 128), (sk, wa, 1, 128), (sv, wa, 2, 128),
-            (ck, wb, 1, 128), (cv, wb, 2, 128), (cq, wb, 3, 128), (up, wf, 0, 512),
+            (so, wb, 0, 128), (ck, wb, 1, 128), (cv, wb, 2, 128), (cq, wb, 3, 128), (co, wb, 4, 128),
+            (up, wf, 0, 512), (down, wf, 1, 512),
         )
     ):
         col = pl.ds(pl.multiple_of(p.t * cols, 128), cols)
-        cp = pltpu.make_async_copy(src, w.at[j, p.z, p.y, :, col], ls.at[i])
+        loads.append(pltpu.make_async_copy(src, w.at[j, p.z, p.y, :, col], ls.at[i]))
+    for i, (src, dst) in enumerate(((x_i, x), (enc_i, enc), (og_i, og))):
+        loads.append(pltpu.make_async_copy(src, dst, ls.at[10 + i]))
+    for cp in loads:
         cp.start()
-        loads.append(cp)
-    for src, w, j, cols in ((so, wb, 0, 128), (co, wb, 4, 128), (down, wf, 1, 512)):
-        col = pl.ds(pl.multiple_of(p.t * cols, 128), cols)
-        w[j, p.z, p.y, :, col] = src[...].astype(F32).T.astype(BF)
-    for cp in loads:
+    p.barrier()
+    GA, GB, GU, GD = G = [
+        Gather(p, w, cols, gss.at[i], grs.at[i])
+        for i, (w, cols) in enumerate(
+            ((wa, 128), (wb, 128), (wf.at[pl.ds(0, 1)], 512), (wf.at[pl.ds(1, 1)], 512))
+        )
+    ]
+    for cp in loads[:3]:
         cp.wait()
-    GA.start()
-    GB.start()
-    GF.start()
+    GA.zs()
+    GA.oxy()
+    for cp in loads[3:]:
+        cp.wait()
+    GB.oxy()
 
     def mat(w, j):
         return w[j].reshape(512, w.shape[4])
@@ -799,20 +904,29 @@
     own = pl.ds(pl.multiple_of(p.c * 512, 128), 512)
     other = pl.ds(pl.multiple_of((1 - p.c) * 512, 128), 512)
     sx = pl.ds(p.x, 1)
-    base = seg[sx, own] * 8
-    high = base + rank[sx, own]
+    ranks = rank[sx, :]
+    codes[1:2, :] = seg[sx, :] * 8
+    codes[0:1, :] = seg[sx, :] * 8 + jnp.concatenate(
+        [jnp.broadcast_to(ranks[:, b : b + 1], (1, 128)) for b in range(8)], axis=1
+    )
+    base, high = codes[1:2, own], codes[0:1, own]
     for i, half in enumerate((own, other)):
-        code = jnp.broadcast_to(seg[sx, half] * 8 + rank[sx, half], (128, 512)).T
+        code = jnp.broadcast_to(codes[0:1, half], (128, 512)).T
         for j in range(4):
             c = code[j * 128 : j * 128 + 128, :1]
             ok = (c >= base) & (c <= high)
             bias[i * 512 + j * 128 : i * 512 + j * 128 + 128, :] = jnp.where(ok, 0.0, -2.0e9)
-
-    GA.plane()
+    tt[...] = turn(x[...])
+
+    GA.plane(GB.zs)
+    GU.oxy()
     GA.corner()
+    GU.zs()
+    GD.oxy()
     GA.cross()
     GB.plane()
     GA.finish()
+    GD.zs()
 
     xv = x[...]
     k1[0:512, :] = nn(xv, mat(wa, 1)).astype(BF)
@@ -826,12 +940,10 @@
     qv = nn(xv, mat(wa, 0)).astype(BF)
     q1[...] = qv
     qt1[...] = turn(qv)
-    GB.corner()
-    GF.plane()
     swap(k1, 0).wait_recv()
     swap(v1, 1).wait_recv()
     vt1[...] = turn(v1[...])
-    attend(qt1, k1, vt1, bias, ot1, l1, gp, {0: GB.cross, 2: GF.corner})
+    attend(qt1, k1, vt1, bias, ot1, l1, gp, {(0, 1): GB.corner, (1, 0): GU.plane, (2, 1): GB.cross, (3, 1): GD.plane})
     o1[...] = turn(ot1[...].astype(BF))
     GB.finish()
     ev = enc[...]
@@ -848,13 +960,14 @@
         h1b[r, :] = (n * g1[...] + b1[...]).astype(BF)
 
     row_steps(512, first)
+    GU.corner()
     qv = nn(h1b[...], mat(wb, 3)).astype(BF)
     q2[...] = qv
     qt2[...] = turn(qv)
     swap(k2, 2).wait_recv()
     swap(v2, 3).wait_recv()
     vt2[...] = turn(v2[...])
-    attend(qt2, k2, vt2, None, ot2, l2, gp, {0: GF.cross})
+    attend(qt2, k2, vt2, None, ot2, l2, gp, {(0, 1): GU.cross, (3, 0): GD.corner})
     o2[...] = turn(ot2[...].astype(BF))
     yb[...] = nt(o2[...], mat(wb, 4))
 
@@ -865,7 +978,8 @@
         h2b[r, :] = (n * g2[...] + b2[...]).astype(BF)
 
     row_steps(512, second)
-    GF.finish()
+    GD.cross()
+    GU.finish()
     hv = h2b[...]
     for j in range(4):
         cols = slice(j * 512, j * 512 + 512)
@@ -879,6 +993,7 @@
             gp[at, :] = cdf + v * (jnp.exp2(v * v * (-0.5 * LOG2E)) * 0.3989422804014327)
 
         row_steps(512, gelu)
+    GD.finish()
     yb[...] = nt(u[...], mat(wf, 1))
 
     def third(r):
@@ -895,33 +1010,35 @@
         low[r, :] = back.astype(BF)
 
     row_steps(512, third)
-    y_copy = pltpu.make_async_copy(yb, y_o, ls.at[7])
+    y_copy = pltpu.make_async_copy(yb, y_o, ls.at[0])
     y_copy.start()
     lv = low[...]
     lowt[...] = turn(lv)
     for j in range(4):
         cols = slice(j * 512, j * 512 + 512)
         dg[:, cols] = (nn(lv, wf[1, :, :, :, cols].reshape(512, 512)) * gp[cols, :]).astype(BF)
-    dz[...] += nt(dg[...], mat(wf, 0))
     for g in G:
         g.drain()
+    RB, RU, RD = R = [
+        Reduce(p, *args, rss.at[i], rrs.at[i])
+        for i, args in enumerate(
+            (
+                (wb, 128, hb, m1, m2, m3, gb_o),
+                (wf.at[pl.ds(0, 1)], 512, hu, u1, u2, u3, gf_o.at[pl.ds(0, 1)]),
+                (wf.at[pl.ds(1, 1)], 512, hd, d1, d2, d3, gf_o.at[pl.ds(1, 1)]),
+            )
+        )
+    ]
+    for j in range(4):
+        cols = slice(j * 512, j * 512 + 512)
+        wf[1, :, :, :, cols] = nn(lowt[...], u[:, cols]).astype(BF).reshape(4, 2, 64, 512)
+    RD.start()
+    dz[...] += nt(dg[...], mat(wf, 0))
     tt[...] = turn(h2b[...])
     for j in range(4):
         cols = slice(j * 512, j * 512 + 512)
         wf[0, :, :, :, cols] = nn(tt[...], dg[:, cols]).astype(BF).reshape(4, 2, 64, 512)
-        wf[1, :, :, :, cols] = nn(lowt[...], u[:, cols]).astype(BF).reshape(4, 2, 64, 512)
-    R = [
-        Reduce(p, *args, rss.at[i], rrs.at[i])
-        for i, args in enumerate(
-            (
-                (ga, 128, ha, a1, a2, a3, ga_o),
-                (wb, 128, hb, m1, m2, m3, gb_o),
-                (wf, 512, hf, f1, f2, f3, gf_o),
-            )
-        )
-    ]
-    RA, RB, RF = R
-    RF.start()
+    RU.start()
 
     def back2(r):
         e = dz[r, :]
@@ -933,6 +1050,7 @@
         low[r, :] = back.astype(BF)
 
     row_steps(512, back2)
+    RD.corner()
     dov = nn(low[...], mat(wb, 4)).astype(BF)
     do[...] = dov
     dot_[...] = turn(dov)
@@ -941,8 +1059,8 @@
     vt2[...] = turn(k2[...])
     attend_back(
         q2, qt2, k2, vt2, v2, do, dot_, ot2, None, l2, dqt,
-        gp.at[pl.ds(0, 512)], gp.at[pl.ds(512, 512)], kvs,
-        {0: RF.corner, 1: RF.plane, 3: RF.along},
+        gp.at[pl.ds(0, 512)], gp.at[pl.ds(512, 512)], kvs, lambda step: step,
+        {(0, 0): RU.corner, (0, 1): RD.plane, (1, 1): RU.plane, (3, 0): RD.along},
     )
 
     def swap_back(buf, i):
@@ -964,6 +1082,7 @@
         low[r, :] = back.astype(BF)
 
     row_steps(512, back1)
+    RU.along()
     dov = nn(low[...], mat(wb, 0)).astype(BF)
     do[...] = dov
     dot_[...] = turn(dov)
@@ -983,30 +1102,72 @@
     join(kvr2, 0)
     y_copy.wait()
     yb[...] = nt(dkv[0], mat(wb, 1)) + nt(dkv[1], mat(wb, 2))
-    e_copy = pltpu.make_async_copy(yb, eg_o, ls.at[7])
+    e_copy = pltpu.make_async_copy(yb, eg_o, ls.at[0])
     e_copy.start()
     tt[...] = turn(enc[...])
     wb[1] = nn(tt[...], dkv[0]).astype(BF).reshape(4, 2, 64, 512)
     wb[2] = nn(tt[...], dkv[1]).astype(BF).reshape(4, 2, 64, 512)
     RB.start()
+    tt[...] = turn(x[...])
+    T = Tail(p, gt, hp, hx, hy, hz, ga_o, aas, ars)
+
+    def order(step):
+        far = (step // 2) * p.x + (1 - step // 2) * (1 - p.x)
+        return 2 * far + step % 2
+
+    def lanes_of(step):
+        return pl.ds(pl.multiple_of(order(step) * 128, 128), 128)
+
+    def part_back(step):
+        at = lanes_of(step)
+        return remote(
+            kvs.at[:, :, at], kvr1.at[:, :, at], ess.at[5 + step], ers.at[5 + step], p.pair
+        )
+
+    def grads(step):
+        at = lanes_of(step)
+        part_back(step).wait_recv()
+
+        def one(r):
+            for i in (0, 1):
+                rows = pl.ds(pl.multiple_of(r.start + 1024 + i * 512, CH), CH)
+                dkv[i, r, at] = (gp[rows, at] + kvr1[i, r, at].astype(F32)).astype(BF)
+
+        row_steps(512, one)
+        dqv = turn(dqt[at, :])
+        dq[:, at] = dqv
+        gt[step, 0] = nn(tt[...], dqv).astype(BF).reshape(4, 2, 64, 128)
+        gt[step, 1] = nn(tt[...], dkv[0, :, at]).astype(BF).reshape(4, 2, 64, 128)
+        gt[step, 2] = nn(tt[...], dkv[1, :, at]).astype(BF).reshape(4, 2, 64, 128)
+        T.start(step)
+
+    def both(*fns):
+        def run():
+            for fn in fns:
+                fn()
+
+        return run
+
     attend_back(
         q1, qt1, k1, vt1, v1, do, dot_, ot1, bias, l1, dqt,
-        gp.at[pl.ds(1024, 512)], gp.at[pl.ds(1536, 512)], kvs,
-        {0: RB.corner, 1: RB.plane, 2: RF.finish, 3: RB.along},
-    )
-    swap_back(kvr1, 5).start()
-    tt[...] = turn(x[...])
-    dqv = turn(dqt[...])
-    ga[0] = nn(tt[...], dqv).astype(BF).reshape(4, 2, 64, 512)
-    dz[...] += nt(dqv, mat(wa, 0))
-    swap_back(kvr1, 5).wait()
-    join(kvr1, 1024)
-    ga[1] = nn(tt[...], dkv[0]).astype(BF).reshape(4, 2, 64, 512)
-    ga[2] = nn(tt[...], dkv[1]).astype(BF).reshape(4, 2, 64, 512)
-    RA.start()
-    dz[...] += nt(dkv[0], mat(wa, 1)) + nt(dkv[1], mat(wa, 2))
-    RA.corner()
-    x_copy = pltpu.make_async_copy(dz, dx_o, ls.at[8])
+        gp.at[pl.ds(1024, 512)], gp.at[pl.ds(1536, 512)], kvs, order,
+        {
+            (0, 0): RB.corner,
+            (0, 1): lambda: part_back(0).start(),
+            (1, 0): both(lambda: grads(0), RB.plane),
+            (1, 1): both(lambda: part_back(1).start(), RD.finish),
+            (2, 0): both(lambda: grads(1), lambda: T.sum_pair(0)),
+            (2, 1): both(lambda: part_back(2).start(), RU.finish),
+            (3, 0): both(lambda: grads(2), lambda: T.sum_pair(1), RB.along),
+            (3, 1): lambda: part_back(3).start(),
+        },
+    )
+    T.sum_pair(2)
+    grads(3)
+    T.sum_pair(3)
+    T.sum_y(2)
+    dz[...] += nt(dq[...], mat(wa, 0)) + nt(dkv[0], mat(wa, 1)) + nt(dkv[1], mat(wa, 2))
+    x_copy = pltpu.make_async_copy(dz, dx_o, ls.at[1])
     x_copy.start()
 
     def squares(r):
@@ -1018,20 +1179,20 @@
         return remote(src, st_r.at[i], tss.at[i], trs.at[i], dev)
 
     stat(0, st, p.pair).start()
-    RA.plane()
-    RB.finish()
+    T.sum_y(3)
     stat(0, st, p.pair).wait()
     st_r[6] = st[...] + st_r[0]
     stat(1, st_r.at[6], p.xn).start()
+    T.finish(2)
+    RB.finish()
     stat(1, st_r.at[6], p.xn).wait()
     st_r[7] = st_r[6] + st_r[1]
     stat(2, st_r.at[7], p.yn).start()
-    RA.along()
     stat(2, st_r.at[7], p.yn).wait()
     st_r[8] = st_r[7] + st_r[2]
     for k in (1, 2, 3):
         stat(2 + k, st_r.at[8], p.zn[k]).start()
-    RA.finish()
+    T.finish(3)
     for k in (1, 2, 3):
         stat(2 + k, st_r.at[8], p.zn[k]).wait()
     total = None
@@ -1046,10 +1207,31 @@
     vs_o[...] = jnp.sqrt(total[6:8] * (1.0 / 16384.0))
     for i in range(4):
         swap((k1, v1, k2, v2)[i], i).wait_send()
+    for step in range(4):
+        part_back(step).wait_send()
     for r in R:
         r.drain()
+    T.drain()
     e_copy.wait()
     x_copy.wait()
+
+
+def place_kernel(*refs):
+    srcs, outs, held, sems = refs[:8], refs[8:23], refs[23:31], refs[31]
+    parts = [held[0], held[1], held[2]] + [held[3].at[i] for i in range(3)]
+    parts += [held[4].at[i] for i in range(5)] + [held[5].at[i] for i in range(2)] + [held[6], held[7]]
+    first = [pltpu.make_async_copy(a, b, sems.at[i]) for i, (a, b) in enumerate(zip(srcs, held))]
+    last = [pltpu.make_async_copy(a, b, sems.at[8 + i]) for i, (a, b) in enumerate(zip(parts, outs))]
+    ends = [(0, 1), (1, 2), (2, 3), (3, 6), (6, 11), (11, 13), (13, 14), (14, 15)]
+    order = (6, 7, 3, 4, 5, 0, 1, 2)
+    for i in order:
+        first[i].start()
+    for i in order:
+        first[i].wait()
+        for cp in last[ends[i][0] : ends[i][1]]:
+            cp.start()
+    for cp in last:
+        cp.wait()
 
 
 def fast_shards(
@@ -1060,7 +1242,6 @@
 ):
     vm = pl.BlockSpec(memory_space=pltpu.VMEM)
     hbm = pl.BlockSpec(memory_space=pl.ANY)
-    ranks = jnp.repeat(context_ranks, BLK, axis=1)
     rows = [
         v.reshape(1, 512)
         for v in (norm1_gain, norm1_bias, norm2_gain, norm2_bias, norm3_gain, norm3_bias)
@@ -1078,7 +1259,7 @@
             [V(2, n, 2, 64, cols), V(2, n, 4, 64, cols), V(3, n, 64, cols)],
         ]
 
-    ra, rb, rf = group(3, 128), group(5, 128), group(2, 512)
+    rb, ru, rd = group(5, 128), group(1, 512), group(1, 512)
 
     def attention():
         return [
@@ -1087,7 +1268,9 @@
         ]
 
     scratch = (
-        [V(3, 4, 2, 64, 512), V(5, 4, 2, 64, 512), V(2, 4, 2, 64, 2048), V(3, 4, 2, 64, 512)]
+        [V(512, 512)] * 3
+        + [V(8, 1024, dtype=jnp.int32)]
+        + [V(3, 4, 2, 64, 512), V(5, 4, 2, 64, 512), V(2, 4, 2, 64, 2048), V(4, 3, 4, 2, 64, 128)]
         + attention()
         + attention()
         + [V(1024, 512, dtype=F32), V(512, 512, dtype=F32), V(512, 512, dtype=F32)]
@@ -1096,17 +1279,18 @@
         + [V(512, 512)] * 4
         + [V(512, 512), V(512, 512), V(2, 512, 512), V(2, 512, 512), V(2, 512, 512), V(2, 512, 512)]
         + [V(512, 512), V(512, 512, dtype=F32), V(512, 128, dtype=F32), V(8, 512, dtype=F32)]
-        + [ra[0], rb[0], rf[0]]
-        + ra[1] + rb[1] + rf[1]
+        + [rb[0], ru[0], rd[0]]
+        + rb[1] + ru[1] + rd[1]
+        + [V(2, 3, 4, 2, 64, 128), V(3, 4, 2, 64, 128), V(3, 4, 64, 128), V(3, 3, 64, 128)]
         + [V(9, 8, 512, dtype=F32)]
-        + [S(3, 17), S(3, 17), S(3, 9), S(3, 9), S(6), S(6), S(6), S(6), S(9)]
+        + [S(4, 17), S(4, 17), S(3, 9), S(3, 9), S(9), S(9), S(9), S(9), S(6), S(6), S(13)]
     )
     big = jax.ShapeDtypeStruct((512, 512), F32)
     outs = pl.pallas_call(
         fast_kernel,
         out_shape=[big, big, big]
         + [jax.ShapeDtypeStruct(s, F32) for s in ((3, 64, 128), (5, 64, 128), (2, 64, 512), (6, 512), (2, 512))],
-        in_specs=[vm] * 6 + [hbm] * 3 + [vm] + [hbm] * 3 + [vm] + [hbm] + [vm] + [vm] * 6,
+        in_specs=[hbm] * 3 + [vm] * 3 + [hbm] * 10 + [vm] * 6,
         out_specs=[hbm] * 3 + [vm] * 5,
         scratch_shapes=scratch,
         compiler_params=pltpu.CompilerParams(
@@ -1114,13 +1298,23 @@
         ),
         name="layer",
     )(
-        tokens, encoder_states, output_grad, valid_mask.reshape(1, 512), segment_ids, ranks,
-        self_query, self_key, self_value, self_output,
-        cross_query, cross_key, cross_value, cross_output, hidden_up, hidden_down, *rows,
-    )
-    y, dx, eg, ga, gb, gf, ns, vs = outs
+        tokens, encoder_states, output_grad, valid_mask.reshape(1, 512), segment_ids, context_ranks,
+        self_query, self_key, self_value, self_output.T,
+        cross_query, cross_key, cross_value, cross_output.T, hidden_up, hidden_down.T, *rows,
+    )
+    ends = [big, big, big] + [jax.ShapeDtypeStruct((64, 128), F32)] * 8
+    ends += [jax.ShapeDtypeStruct((64, 512), F32)] * 2
+    ends += [jax.ShapeDtypeStruct(v, F32) for v in ((6, 512), (2, 512))]
+    y, dx, eg, dsq, dsk, dsv, dso, dck, dcv, dcq, dco, dup, ddown, ns, vs = pl.pallas_call(
+        place_kernel,
+        out_shape=ends,
+        in_specs=[hbm] * 8,
+        out_specs=[hbm] * 15,
+        scratch_shapes=[pltpu.VMEM(o.shape, F32) for o in outs] + [S(23)],
+        name="place",
+    )(*outs)
     return (
-        y, dx, eg, ga[0], ga[1], ga[2], gb[0].T, gb[3], gb[1], gb[2], gb[4].T, gf[0], gf[1].T, ns, vs,
+        y, dx, eg, dsq, dsk, dsv, dso.T, dcq, dck, dcv, dco.T, dup, ddown.T, ns, vs,
     )
 
 

time: 160 us -> 137 us (0.86)
  local copies, waits for them, and re-layouts: 12.3 us -> 0 us
  Pallas kernels: 146 us -> 136 us
    pallas_call x1, Pallas kernels: 146 us -> 132 us  [fast_shards(): pl.pallas_call(fast_kernel, out_shape=[big, big, big] + [jax.ShapeDtypeSt...]
    unnamed x28 -> x0, local copies, waits for them, and re-layouts: 8.99 us -> none
    pallas_call x0 -> x1, Pallas kernels: none -> 3.49 us  [fast_shards(): pl.pallas_call(place_kernel, out_shape=ends, in_specs=[hbm] * 8, out_spec...]
    transpose x2 -> x0, local copies, waits for them, and re-layouts: 3.34 us -> none  [the longest x1 1.68 us: fast_shards(): gf[1]]
where the time goes in v2:
time: 137 us; the launch traced here: 136 us
  Pallas kernels  136 us (99%)
    pallas_call x1, Pallas kernels, fast_shards(): pl.pallas_call(fast_kernel, out_shape=[big, big, big] + [jax.ShapeDtypeSt...  132 us
    pallas_call x1, Pallas kernels, fast_shards(): pl.pallas_call(place_kernel, out_shape=ends, in_specs=[hbm] * 8, out_spec...  3.49 us

profile of v2, /device:TPU:0, one launch (start us, length us, event | category | flops | bytes accessed | tf_op | source)
XLA Modules:
  0.0 136.4 jit_solution(577446605825376049)
XLA Ops:
  0.7 132.0 %layer.1 = (f32[512,512]{1,0:T(8,128)}, f32[512,512]{1,0:T(8,128)}, f32[512,512]{1,0:T(8,128)}, f32[3,64,128]{2,1,0:T(8,128)}, f32[5,64,128]{2,1,0:T(8,128)}, /*...) custom-call(bf16[512,512]{1,0:T(8,128)(2,1)} %x_i.1, bf16[512,512]{1,0:T(8,128)(2,1)} %enc_i.1, ...), custom_call_target="tpu_custom_call" | custom-call | tf_op jit(solution)/shard_map/layer/pallas_call | solution.py:1289
  132.7 3.5 %place.1 = (f32[512,512]{1,0:T(8,128)}, f32[512,512]{1,0:T(8,128)}, f32[512,512]{1,0:T(8,128)}, f32[64,128]{1,0:T(8,128)}, f32[64,128]{1,0:T(8,128)}, /*index=5*...) custom-call(f32[512,512]{1,0:T(8,128)} %get-tuple-element.38.refs_0_, ...), custom_call_target="tpu_custom_call" | custom-call | tf_op jit(solution)/shard_map/place/pallas_call | solution.py:1308

commit v3 on v2

--- a/solution.py
+++ b/solution.py
@@ -402,7 +402,7 @@
 F32 = jnp.float32
 LOG2E = 1.4426950408889634
 SCALE = 0.125 * LOG2E
-CH = 128
+CH = 256
 
 
 def nn(a, b):
@@ -428,6 +428,8 @@
         self.yn = (self.z * 2 + 1 - self.y, self.t)
         self.pair = (self.d, self.x * 2 + 1 - self.c)
         self.zn = [None] + [((((self.z + k) % 4) * 2 + self.y), self.t) for k in (1, 2, 3)]
+        top = self.z // 2
+        self.near = [self.z, top * (5 - self.z) + (1 - top) * (1 - self.z), 2 - top, 3 * (1 - top)]
 
     def barrier(self):
         sem = pltpu.get_barrier_semaphore()
@@ -450,20 +452,23 @@
         return pl.ds(pl.multiple_of(t * self.cols, 128), self.cols)
 
     def blk(self, k, y, t):
-        zs = (self.p.z - k + 4) % 4
-        return self.w.at[:, zs, y, :, self.col(t)]
-
-    def cp(self, ref, i, dev):
-        return remote(ref, ref, self.ss.at[i], self.rs.at[i], dev)
+        return self.w.at[:, self.p.near[k], y, :, self.col(t)]
+
+    def cp(self, ref, i, dev, send=None):
+        return remote(ref, ref, self.ss.at[i if send is None else send], self.rs.at[i], dev)
 
     def own(self):
         return self.blk(0, self.p.y, self.p.t)
 
     def z_send(self, k):
-        return self.cp(self.own(), k - 1, self.p.zn[k])
+        p = self.p
+        dev = (p.near[k] * 2 + p.y, p.t)
+        return self.cp(self.own(), 15 + p.z, dev, k - 1)
 
     def z_recv(self, k):
-        return self.cp(self.blk(k, self.p.y, self.p.t), k - 1, self.p.zn[k])
+        p = self.p
+        ref = self.blk(k, p.y, p.t)
+        return self.cp(ref, 15 + p.near[k], (p.near[k] * 2 + p.y, p.t), k - 1)
 
     def x_send(self, k):
         return self.cp(self.blk(k, self.p.y, self.p.t), 3 + k, self.p.xn)
@@ -490,10 +495,10 @@
         return self.w.at[:, :, :, :, self.col(x * 2 + core)]
 
     def p_send(self, i):
-        return self.cp(self.rail(i, self.p.c), 15 + i, self.p.pair)
+        return self.cp(self.rail(i, self.p.c), 1 + i, self.p.pair, 17 + i)
 
     def p_recv(self, i):
-        return self.cp(self.rail(i, 1 - self.p.c), 15 + i, self.p.pair)
+        return self.cp(self.rail(i, 1 - self.p.c), 1 + i, self.p.pair, 17 + i)
 
     def zs(self):
         for k in (1, 2, 3):
@@ -759,36 +764,43 @@
 
 
 def attend(qt, k, vt, bias, ot, lse, temp, hooks):
-    def pair(p, _):
+    def ready(p, h):
         lanes = pl.ds(pl.multiple_of(p * 128, 128), 128)
-        kp = k[:, lanes]
-        qp = qt[lanes, :]
+        return k[:, lanes], keep_half(qt[lanes, :], 0, h)
+
+    def score(kp, qm, h, i, top):
+        s = nn(kp[i * 512 : i * 512 + 512], qm) * SCALE
+        if bias is not None:
+            s = s + bias[i * 512 : i * 512 + 512, :]
+        temp[h * 1024 + i * 512 : h * 1024 + i * 512 + 512, :] = s
+        m = jnp.max(s, axis=0, keepdims=True)
+        return m if top is None else jnp.maximum(top, m)
+
+    def mix(vh, h, i, top, total, mixed):
+        e = jnp.exp2(temp[h * 1024 + i * 512 : h * 1024 + i * 512 + 512, :] - top)
+        part = jnp.sum(e, axis=0, keepdims=True)
+        o = nn(vh[:, i * 512 : i * 512 + 512], e.astype(BF))
+        return (part, o) if total is None else (total + part, mixed + o)
+
+    def pair(p, top):
         for h in (0, 1):
-            qm = keep_half(qp, 0, h)
-            top = None
-            for i in range(4):
-                rows = slice(i * 256, i * 256 + 256)
-                s = nn(kp[rows], qm) * SCALE
-                if bias is not None:
-                    s = s + bias[rows, :]
-                temp[rows, :] = s
-                m = jnp.max(s, axis=0, keepdims=True)
-                top = m if top is None else jnp.maximum(top, m)
-            total, mixed = None, None
+            kp, qm = ready(p if h == 0 else (p + 1) % 4, 1 - h)
             vh = vt[pl.ds(pl.multiple_of(p * 128 + h * 64, 64), 64), :]
-            for i in range(4):
-                rows = slice(i * 256, i * 256 + 256)
-                e = jnp.exp2(temp[rows, :] - top)
-                part = jnp.sum(e, axis=0, keepdims=True)
-                total = part if total is None else total + part
-                o = nn(vh[:, rows], e.astype(BF))
-                mixed = o if mixed is None else mixed + o
+            total = mixed = later = None
+            for i in range(2):
+                later = score(kp, qm, 1 - h, i, later)
+                total, mixed = mix(vh, h, i, top, total, mixed)
             ot[pl.ds(pl.multiple_of(p * 128 + h * 64, 64), 64), :] = mixed * (1.0 / total)
             lse[pl.ds(p * 2 + h, 1), :] = top + jnp.log2(total)
+            top = later
             run_hooks(hooks, p, h)
-        return 0
-
-    lax.fori_loop(0, 4, pair, 0)
+        return top
+
+    kp, qm = ready(0, 0)
+    top = None
+    for i in range(2):
+        top = score(kp, qm, 0, i, top)
+    lax.fori_loop(0, 4, pair, top)
 
 
 def attend_back(q, qt, k, kt, v, do, dot_, ot, bias, lse, dqt, dk_own, dv_own, dkv_send, order, hooks):
@@ -804,33 +816,49 @@
         dor = jnp.concatenate([keep_half(do[:, lanes], 1, h) for h in (0, 1)], axis=0)
         ds_sum = [jnp.sum(inner[h * 64 : h * 64 + 64], axis=0, keepdims=True) for h in (0, 1)]
         logs = [lse[pl.ds(p * 2 + h, 1), :] for h in (0, 1)]
+        shares, grads = {}, {}
         dq = [None, None]
-        for i in range(4):
+        dvs, dks = {}, {}
+
+        def one(h, i):
             rows = slice(i * 256, i * 256 + 256)
-            shares, grads = [], []
-            for h in (0, 1):
-                s = nn(kp[rows], qms[h]) * SCALE
-                if bias is not None:
-                    s = s + bias[rows, :]
-                e = jnp.exp2(s - logs[h])
-                dp = nn(vp[rows], doms[h])
-                g = (e * (dp - ds_sum[h])).astype(BF)
-                shares.append(e.astype(BF))
-                grads.append(g)
-                kh = kt[pl.ds(pl.multiple_of(p * 128 + h * 64, 64), 64), rows]
-                part = nn(kh, g)
-                dq[h] = part if dq[h] is None else dq[h] + part
-            dv = nn(jnp.concatenate(shares, axis=1), dor)
-            dk = nn(jnp.concatenate(grads, axis=1), qr) * 0.125
+            s = nn(kp[rows], qms[h]) * SCALE
+            if bias is not None:
+                s = s + bias[rows, :]
+            e = jnp.exp2(s - logs[h])
+            dp = nn(vp[rows], doms[h])
+            shares[h, i] = e.astype(BF)
+            grads[h, i] = (e * (dp - ds_sum[h])).astype(BF)
+
+        def two(h, i):
+            rows = slice(i * 256, i * 256 + 256)
+            kh = kt[pl.ds(pl.multiple_of(p * 128 + h * 64, 64), 64), rows]
+            part = nn(kh, grads[h, i])
+            dq[h] = part if dq[h] is None else dq[h] + part
+            dv = nn(shares[h, i], dor[h * 512 : h * 512 + 512])
+            dk = nn(grads[h, i], qr[h * 512 : h * 512 + 512])
+            dvs[i] = dv if i not in dvs else dvs[i] + dv
+            dks[i] = dk if i not in dks else dks[i] + dk
+
+        def out(i):
+            rows = slice(i * 256, i * 256 + 256)
             if i < 2:
-                dk_own[rows, lanes] = dk
-                dv_own[rows, lanes] = dv
+                dk_own[rows, lanes] = dks[i] * 0.125
+                dv_own[rows, lanes] = dvs[i]
             else:
                 back = slice(i * 256 - 512, i * 256 - 256)
-                dkv_send[0, back, lanes] = dk.astype(BF)
-                dkv_send[1, back, lanes] = dv.astype(BF)
-            if i == 1:
-                run_hooks(hooks, step, 0)
+                dkv_send[0, back, lanes] = (dks[i] * 0.125).astype(BF)
+                dkv_send[1, back, lanes] = dvs[i].astype(BF)
+
+        for i in range(4):
+            one(0, i)
+        for i in range(4):
+            one(1, i)
+            two(0, i)
+        run_hooks(hooks, step, 0)
+        for i in range(4):
+            two(1, i)
+            out(i)
         for h in (0, 1):
             dqt[pl.ds(pl.multiple_of(p * 128 + h * 64, 64), 64), :] = (dq[h] * 0.125).astype(BF)
         run_hooks(hooks, step, 1)
@@ -861,17 +889,19 @@
     x, enc, og, codes, wa, wb, wf, gt,
     q1, qt1, k1, v1, vt1, o1, ot1, l1,
     q2, qt2, k2, v2, vt2, o2, ot2, l2,
-    bias, n1, n2, r1, r2, h1b, h2b, u, gp, dg, dz, low, lowt, do, dot_,
-    dqt, dq, kvs, kvr1, kvr2, dkv, tt, yb, vcol, st,
-    hb, hu, hd, m1, m2, m3, u1, u2, u3, d1, d2, d3, hp, hx, hy, hz,
+    bias, n1, n2, h1b, h2b, u, gp, dg, dz, low, lowt, do, dot_,
+    kvs, kvr1, kvr2, tt, yb, row, st,
+    hc, hq, hu, hd, c1, c2, c3, p1, p2, p3, u1, u2, u3, d1, d2, d3, hp, hx, hy, hz,
     st_r, gss, grs, rss, rrs, aas, ars, ess, ers, tss, trs, ls,
 ):
+    dqt, dq = h2b, q2
+    dkv = [v2.at[pl.ds(0, 512)], v2.at[pl.ds(512, 512)]]
     p = Place()
     loads = []
     for i, (src, w, j, cols) in enumerate(
         (
             (sq, wa, 0, 128), (sk, wa, 1, 128), (sv, wa, 2, 128),
-            (so, wb, 0, 128), (ck, wb, 1, 128), (cv, wb, 2, 128), (cq, wb, 3, 128), (co, wb, 4, 128),
+            (so, wb, 0, 128), (co, wb, 1, 128), (cq, wb, 2, 128), (ck, wb, 3, 128), (cv, wb, 4, 128),
             (up, wf, 0, 512), (down, wf, 1, 512),
         )
     ):
@@ -900,7 +930,7 @@
         return w[j].reshape(512, w.shape[4])
 
     st[...] = jnp.zeros_like(st)
-    vcol[...] = jnp.broadcast_to(valid[...].astype(F32), (128, 512)).T
+    row[...] = jnp.broadcast_to(valid[...].astype(F32), (128, 512)).T
     own = pl.ds(pl.multiple_of(p.c * 512, 128), 512)
     other = pl.ds(pl.multiple_of((1 - p.c) * 512, 128), 512)
     sx = pl.ds(p.x, 1)
@@ -943,63 +973,70 @@
     swap(k1, 0).wait_recv()
     swap(v1, 1).wait_recv()
     vt1[...] = turn(v1[...])
-    attend(qt1, k1, vt1, bias, ot1, l1, gp, {(0, 1): GB.corner, (1, 0): GU.plane, (2, 1): GB.cross, (3, 1): GD.plane})
+    attend(qt1, k1, vt1, bias, ot1, l1, gp, {(0, 0): GB.corner, (1, 0): GU.plane, (2, 0): GB.cross, (3, 0): GD.plane})
     o1[...] = turn(ot1[...].astype(BF))
     GB.finish()
     ev = enc[...]
-    k2[0:512, :] = nn(ev, mat(wb, 1)).astype(BF)
-    v2[0:512, :] = nn(ev, mat(wb, 2)).astype(BF)
+    k2[0:512, :] = nn(ev, mat(wb, 3)).astype(BF)
+    v2[0:512, :] = nn(ev, mat(wb, 4)).astype(BF)
     swap(k2, 2).start()
     swap(v2, 3).start()
     yb[...] = nt(o1[...], mat(wb, 0))
+    GU.corner()
 
     def first(r):
         n, s = norm_rows(x[r, :].astype(F32) + yb[r, :])
         n1[r, :] = n
-        r1[r, :] = s
+        row[r, 0:1] = s
         h1b[r, :] = (n * g1[...] + b1[...]).astype(BF)
 
     row_steps(512, first)
-    GU.corner()
-    qv = nn(h1b[...], mat(wb, 3)).astype(BF)
+    qv = nn(h1b[...], mat(wb, 2)).astype(BF)
     q2[...] = qv
     qt2[...] = turn(qv)
     swap(k2, 2).wait_recv()
     swap(v2, 3).wait_recv()
     vt2[...] = turn(v2[...])
-    attend(qt2, k2, vt2, None, ot2, l2, gp, {(0, 1): GU.cross, (3, 0): GD.corner})
+    attend(qt2, k2, vt2, None, ot2, l2, gp, {(0, 1): GD.corner, (2, 1): GU.cross})
     o2[...] = turn(ot2[...].astype(BF))
-    yb[...] = nt(o2[...], mat(wb, 4))
+    yb[...] = nt(o2[...], mat(wb, 1))
 
     def second(r):
         n, s = norm_rows(n1[r, :] * g1[...] + b1[...] + yb[r, :])
         n2[r, :] = n
-        r2[r, :] = s
+        row[r, 1:2] = s
         h2b[r, :] = (n * g2[...] + b2[...]).astype(BF)
 
     row_steps(512, second)
-    GD.cross()
-    GU.finish()
     hv = h2b[...]
-    for j in range(4):
-        cols = slice(j * 512, j * 512 + 512)
+    blocks = [p.t, p.pair[1], p.xt, (1 - p.x) * 2 + 1 - p.c]
+    waits = [None, GU.p_recv(0).wait_recv, GD.cross, GU.p_recv(1).wait_recv]
+    for t, wait in zip(blocks, waits):
+        if wait is not None:
+            wait()
+        cols = pl.ds(pl.multiple_of(t * 512, 512), 512)
         gp[cols, :] = nn(hv, wf[0, :, :, :, cols].reshape(512, 512))
 
-        def gelu(r, j=j, cols=cols):
-            at = pl.ds(pl.multiple_of(r.start + j * 512, CH), CH)
+        def gelu(r, cols=cols, t=t):
+            at = pl.ds(pl.multiple_of(r.start + t * 512, CH), CH)
             v = gp[at, :]
             cdf = 0.5 * (1.0 + lax.erf(v * 0.7071067811865476))
             u[r, cols] = (v * cdf).astype(BF)
             gp[at, :] = cdf + v * (jnp.exp2(v * v * (-0.5 * LOG2E)) * 0.3989422804014327)
 
         row_steps(512, gelu)
-    GD.finish()
-    yb[...] = nt(u[...], mat(wf, 1))
+    waits = [None, GD.p_recv(0).wait_recv, None, GD.p_recv(1).wait_recv]
+    for i, (t, wait) in enumerate(zip(blocks, waits)):
+        if wait is not None:
+            wait()
+        cols = pl.ds(pl.multiple_of(t * 512, 512), 512)
+        part = nt(u[:, cols], wf[1, :, :, :, cols].reshape(512, 512))
+        yb[...] = part if i == 0 else yb[...] + part
 
     def third(r):
         n, s = norm_rows(n2[r, :] * g2[...] + b2[...] + yb[r, :])
         out = n * g3[...] + b3[...]
-        vc = vcol[r, :1]
+        vc = row[r, 2:3]
         yb[r, :] = out
         e = og[r, :].astype(F32) * vc
         st[4:5, :] += jnp.sum(e * n, axis=0, keepdims=True)
@@ -1019,13 +1056,14 @@
         dg[:, cols] = (nn(lv, wf[1, :, :, :, cols].reshape(512, 512)) * gp[cols, :]).astype(BF)
     for g in G:
         g.drain()
-    RB, RU, RD = R = [
-        Reduce(p, *args, rss.at[i], rrs.at[i])
-        for i, args in enumerate(
+    RC, RP, RU, RD = R = [
+        Reduce(p, w.at[pl.ds(at, n)], cols, *bufs, out.at[pl.ds(at, n)], rss.at[i], rrs.at[i])
+        for i, (w, at, n, cols, bufs, out) in enumerate(
             (
-                (wb, 128, hb, m1, m2, m3, gb_o),
-                (wf.at[pl.ds(0, 1)], 512, hu, u1, u2, u3, gf_o.at[pl.ds(0, 1)]),
-                (wf.at[pl.ds(1, 1)], 512, hd, d1, d2, d3, gf_o.at[pl.ds(1, 1)]),
+                (wb, 0, 2, 128, (hc, c1, c2, c3), gb_o),
+                (wb, 2, 3, 128, (hq, p1, p2, p3), gb_o),
+                (wf, 0, 1, 512, (hu, u1, u2, u3), gf_o),
+                (wf, 1, 1, 512, (hd, d1, d2, d3), gf_o),
             )
         )
     ]
@@ -1039,28 +1077,29 @@
         cols = slice(j * 512, j * 512 + 512)
         wf[0, :, :, :, cols] = nn(tt[...], dg[:, cols]).astype(BF).reshape(4, 2, 64, 512)
     RU.start()
+    RD.corner()
 
     def back2(r):
         e = dz[r, :]
         n = n2[r, :]
         st[2:3, :] += jnp.sum(e * n, axis=0, keepdims=True)
         st[3:4, :] += jnp.sum(e, axis=0, keepdims=True)
-        back = norm_back_rows(e, n, r2[r, :], g2[...])
+        back = norm_back_rows(e, n, row[r, 1:2], g2[...])
         dz[r, :] = back
         low[r, :] = back.astype(BF)
 
     row_steps(512, back2)
-    RD.corner()
-    dov = nn(low[...], mat(wb, 4)).astype(BF)
+    dov = nn(low[...], mat(wb, 1)).astype(BF)
     do[...] = dov
     dot_[...] = turn(dov)
     lowt[...] = turn(low[...])
-    wb[4] = nn(lowt[...], o2[...]).astype(BF).reshape(4, 2, 64, 512)
+    wb[1] = nn(lowt[...], o2[...]).astype(BF).reshape(4, 2, 64, 512)
     vt2[...] = turn(k2[...])
+    RU.corner()
     attend_back(
         q2, qt2, k2, vt2, v2, do, dot_, ot2, None, l2, dqt,
         gp.at[pl.ds(0, 512)], gp.at[pl.ds(512, 512)], kvs, lambda step: step,
-        {(0, 0): RU.corner, (0, 1): RD.plane, (1, 1): RU.plane, (3, 0): RD.along},
+        {(0, 0): RD.plane, (1, 0): RU.plane, (3, 0): RD.along},
     )
 
     def swap_back(buf, i):
@@ -1068,16 +1107,37 @@
 
     swap_back(kvr2, 4).start()
     dqv = turn(dqt[...])
-    dz[...] += nt(dqv, mat(wb, 3))
+    dz[...] += nt(dqv, mat(wb, 2))
     tt[...] = turn(h1b[...])
-    wb[3] = nn(tt[...], dqv).astype(BF).reshape(4, 2, 64, 512)
+    wb[2] = nn(tt[...], dqv).astype(BF).reshape(4, 2, 64, 512)
+    tt[...] = turn(enc[...])
+    swap_back(kvr2, 4).wait()
+    for i in range(4):
+        swap((k1, v1, k2, v2)[i], i).wait_send()
+
+    def join(recv, at):
+        def one(r):
+            for i in (0, 1):
+                own_rows = pl.ds(pl.multiple_of(r.start + at + i * 512, CH), CH)
+                dkv[i][r, :] = (gp[own_rows, :] + recv[i, r, :].astype(F32)).astype(BF)
+
+        row_steps(512, one)
+
+    join(kvr2, 0)
+    y_copy.wait()
+    yb[...] = nt(dkv[0][...], mat(wb, 3)) + nt(dkv[1][...], mat(wb, 4))
+    e_copy = pltpu.make_async_copy(yb, eg_o, ls.at[0])
+    e_copy.start()
+    wb[3] = nn(tt[...], dkv[0][...]).astype(BF).reshape(4, 2, 64, 512)
+    wb[4] = nn(tt[...], dkv[1][...]).astype(BF).reshape(4, 2, 64, 512)
+    RP.start()
 
     def back1(r):
         e = dz[r, :]
         n = n1[r, :]
         st[0:1, :] += jnp.sum(e * n, axis=0, keepdims=True)
         st[1:2, :] += jnp.sum(e, axis=0, keepdims=True)
-        back = norm_back_rows(e, n, r1[r, :], g1[...])
+        back = norm_back_rows(e, n, row[r, 0:1], g1[...])
         dz[r, :] = back
         low[r, :] = back.astype(BF)
 
@@ -1088,26 +1148,9 @@
     dot_[...] = turn(dov)
     lowt[...] = turn(low[...])
     wb[0] = nn(lowt[...], o1[...]).astype(BF).reshape(4, 2, 64, 512)
+    RC.start()
+    RP.corner()
     vt1[...] = turn(k1[...])
-    swap_back(kvr2, 4).wait()
-
-    def join(recv, at):
-        def one(r):
-            for i in (0, 1):
-                own_rows = pl.ds(pl.multiple_of(r.start + at + i * 512, CH), CH)
-                dkv[i, r, :] = (gp[own_rows, :] + recv[i, r, :].astype(F32)).astype(BF)
-
-        row_steps(512, one)
-
-    join(kvr2, 0)
-    y_copy.wait()
-    yb[...] = nt(dkv[0], mat(wb, 1)) + nt(dkv[1], mat(wb, 2))
-    e_copy = pltpu.make_async_copy(yb, eg_o, ls.at[0])
-    e_copy.start()
-    tt[...] = turn(enc[...])
-    wb[1] = nn(tt[...], dkv[0]).astype(BF).reshape(4, 2, 64, 512)
-    wb[2] = nn(tt[...], dkv[1]).astype(BF).reshape(4, 2, 64, 512)
-    RB.start()
     tt[...] = turn(x[...])
     T = Tail(p, gt, hp, hx, hy, hz, ga_o, aas, ars)
 
@@ -1131,14 +1174,14 @@
         def one(r):
             for i in (0, 1):
                 rows = pl.ds(pl.multiple_of(r.start + 1024 + i * 512, CH), CH)
-                dkv[i, r, at] = (gp[rows, at] + kvr1[i, r, at].astype(F32)).astype(BF)
+                dkv[i][r, at] = (gp[rows, at] + kvr1[i, r, at].astype(F32)).astype(BF)
 
         row_steps(512, one)
         dqv = turn(dqt[at, :])
         dq[:, at] = dqv
         gt[step, 0] = nn(tt[...], dqv).astype(BF).reshape(4, 2, 64, 128)
-        gt[step, 1] = nn(tt[...], dkv[0, :, at]).astype(BF).reshape(4, 2, 64, 128)
-        gt[step, 2] = nn(tt[...], dkv[1, :, at]).astype(BF).reshape(4, 2, 64, 128)
+        gt[step, 1] = nn(tt[...], dkv[0][:, at]).astype(BF).reshape(4, 2, 64, 128)
+        gt[step, 2] = nn(tt[...], dkv[1][:, at]).astype(BF).reshape(4, 2, 64, 128)
         T.start(step)
 
     def both(*fns):
@@ -1152,26 +1195,26 @@
         q1, qt1, k1, vt1, v1, do, dot_, ot1, bias, l1, dqt,
         gp.at[pl.ds(1024, 512)], gp.at[pl.ds(1536, 512)], kvs, order,
         {
-            (0, 0): RB.corner,
-            (0, 1): lambda: part_back(0).start(),
-            (1, 0): both(lambda: grads(0), RB.plane),
-            (1, 1): both(lambda: part_back(1).start(), RD.finish),
+            (0, 0): RC.corner,
+            (0, 1): both(lambda: part_back(0).start(), RP.plane),
+            (1, 0): lambda: grads(0),
+            (1, 1): both(lambda: part_back(1).start(), RC.plane, RD.finish),
             (2, 0): both(lambda: grads(1), lambda: T.sum_pair(0)),
-            (2, 1): both(lambda: part_back(2).start(), RU.finish),
-            (3, 0): both(lambda: grads(2), lambda: T.sum_pair(1), RB.along),
-            (3, 1): lambda: part_back(3).start(),
+            (2, 1): both(lambda: part_back(2).start(), RP.along, RU.finish),
+            (3, 0): both(lambda: grads(2), lambda: T.sum_pair(1)),
+            (3, 1): both(lambda: part_back(3).start(), RC.along),
         },
     )
     T.sum_pair(2)
     grads(3)
     T.sum_pair(3)
     T.sum_y(2)
-    dz[...] += nt(dq[...], mat(wa, 0)) + nt(dkv[0], mat(wa, 1)) + nt(dkv[1], mat(wa, 2))
+    dz[...] += nt(dq[...], mat(wa, 0)) + nt(dkv[0][...], mat(wa, 1)) + nt(dkv[1][...], mat(wa, 2))
     x_copy = pltpu.make_async_copy(dz, dx_o, ls.at[1])
     x_copy.start()
 
     def squares(r):
-        st[7:8, :] += jnp.sum(vcol[r, :1] * dz[r, :] * dz[r, :], axis=0, keepdims=True)
+        st[7:8, :] += jnp.sum(row[r, 2:3] * dz[r, :] * dz[r, :], axis=0, keepdims=True)
 
     row_steps(512, squares)
 
@@ -1184,7 +1227,8 @@
     st_r[6] = st[...] + st_r[0]
     stat(1, st_r.at[6], p.xn).start()
     T.finish(2)
-    RB.finish()
+    RP.finish()
+    RC.finish()
     stat(1, st_r.at[6], p.xn).wait()
     st_r[7] = st_r[6] + st_r[1]
     stat(2, st_r.at[7], p.yn).start()
@@ -1205,8 +1249,6 @@
         total = part if total is None else total + part
     ns_o[...] = total[0:6]
     vs_o[...] = jnp.sqrt(total[6:8] * (1.0 / 16384.0))
-    for i in range(4):
-        swap((k1, v1, k2, v2)[i], i).wait_send()
     for step in range(4):
         part_back(step).wait_send()
     for r in R:
@@ -1259,7 +1301,7 @@
             [V(2, n, 2, 64, cols), V(2, n, 4, 64, cols), V(3, n, 64, cols)],
         ]
 
-    rb, ru, rd = group(5, 128), group(1, 512), group(1, 512)
+    rc, rp, ru, rd = group(2, 128), group(3, 128), group(1, 512), group(1, 512)
 
     def attention():
         return [
@@ -1274,16 +1316,16 @@
         + attention()
         + attention()
         + [V(1024, 512, dtype=F32), V(512, 512, dtype=F32), V(512, 512, dtype=F32)]
-        + [V(512, 1, dtype=F32), V(512, 1, dtype=F32), V(512, 512), V(512, 512)]
+        + [V(512, 512), V(512, 512)]
         + [V(512, 2048), V(2048, 512, dtype=F32), V(512, 2048), V(512, 512, dtype=F32)]
         + [V(512, 512)] * 4
-        + [V(512, 512), V(512, 512), V(2, 512, 512), V(2, 512, 512), V(2, 512, 512), V(2, 512, 512)]
+        + [V(2, 512, 512), V(2, 512, 512), V(2, 512, 512)]
         + [V(512, 512), V(512, 512, dtype=F32), V(512, 128, dtype=F32), V(8, 512, dtype=F32)]
-        + [rb[0], ru[0], rd[0]]
-        + rb[1] + ru[1] + rd[1]
+        + [rc[0], rp[0], ru[0], rd[0]]
+        + rc[1] + rp[1] + ru[1] + rd[1]
         + [V(2, 3, 4, 2, 64, 128), V(3, 4, 2, 64, 128), V(3, 4, 64, 128), V(3, 3, 64, 128)]
         + [V(9, 8, 512, dtype=F32)]
-        + [S(4, 17), S(4, 17), S(3, 9), S(3, 9), S(9), S(9), S(9), S(9), S(6), S(6), S(13)]
+        + [S(4, 19), S(4, 19), S(4, 9), S(4, 9), S(9), S(9), S(9), S(9), S(6), S(6), S(13)]
     )
     big = jax.ShapeDtypeStruct((512, 512), F32)
     outs = pl.pallas_call(
@@ -1294,7 +1336,7 @@
         out_specs=[hbm] * 3 + [vm] * 5,
         scratch_shapes=scratch,
         compiler_params=pltpu.CompilerParams(
-            collective_id=0, has_side_effects=True, vmem_limit_bytes=60 << 20
+            collective_id=0, has_side_effects=True, vmem_limit_bytes=63 << 20
         ),
         name="layer",
     )(
@@ -1305,7 +1347,7 @@
     ends = [big, big, big] + [jax.ShapeDtypeStruct((64, 128), F32)] * 8
     ends += [jax.ShapeDtypeStruct((64, 512), F32)] * 2
     ends += [jax.ShapeDtypeStruct(v, F32) for v in ((6, 512), (2, 512))]
-    y, dx, eg, dsq, dsk, dsv, dso, dck, dcv, dcq, dco, dup, ddown, ns, vs = pl.pallas_call(
+    y, dx, eg, dsq, dsk, dsv, dso, dco, dcq, dck, dcv, dup, ddown, ns, vs = pl.pallas_call(
         place_kernel,
         out_shape=ends,
         in_specs=[hbm] * 8,

time: 137 us -> 123 us (0.90)
  Pallas kernels: 136 us -> 122 us
    pallas_call x1, Pallas kernels: 132 us -> 118 us  [fast_shards(): pl.pallas_call(fast_kernel, out_shape=[big, big, big] + [jax.ShapeDtypeSt...]
where the time goes in v3:
time: 123 us
  Pallas kernels  122 us (99%)
    pallas_call x1, Pallas kernels, fast_shards(): pl.pallas_call(fast_kernel, out_shape=[big, big, big] + [jax.ShapeDtypeSt...  118 us
    pallas_call x1, Pallas kernels, fast_shards(): pl.pallas_call(place_kernel, out_shape=ends, in_specs=[hbm] * 8, out_spec...  3.49 us

profile of v3, /device:TPU:0, one launch (start us, length us, event | category | flops | bytes accessed | tf_op | source)
XLA Modules:
  0.0 122.7 jit_solution(4262552112322939552)
XLA Ops:
  0.7 118.3 %layer.1 = (f32[512,512]{1,0:T(8,128)}, f32[512,512]{1,0:T(8,128)}, f32[512,512]{1,0:T(8,128)}, f32[3,64,128]{2,1,0:T(8,128)}, f32[5,64,128]{2,1,0:T(8,128)}, /*...) custom-call(bf16[512,512]{1,0:T(8,128)(2,1)} %x_i.1, bf16[512,512]{1,0:T(8,128)(2,1)} %enc_i.1, ...), custom_call_target="tpu_custom_call" | custom-call | tf_op jit(solution)/shard_map/layer/pallas_call | solution.py:1331
  119.0 3.5 %place.1 = (f32[512,512]{1,0:T(8,128)}, f32[512,512]{1,0:T(8,128)}, f32[512,512]{1,0:T(8,128)}, f32[64,128]{1,0:T(8,128)}, f32[64,128]{1,0:T(8,128)}, /*index=5*...) custom-call(f32[512,512]{1,0:T(8,128)} %get-tuple-element.38.refs_0_, ...), custom_call_target="tpu_custom_call" | custom-call | tf_op jit(solution)/shard_map/place/pallas_call | solution.py:1350

commit v4 on v3

--- a/solution.py
+++ b/solution.py
@@ -431,11 +431,15 @@
         top = self.z // 2
         self.near = [self.z, top * (5 - self.z) + (1 - top) * (1 - self.z), 2 - top, 3 * (1 - top)]
 
+    def plane_peer(self, i):
+        x, y, c = (self.x + i // 4) % 2, (self.y + i // 2) % 2, (self.c + i) % 2
+        return (self.z * 2 + y, x * 2 + c)
+
     def barrier(self):
         sem = pltpu.get_barrier_semaphore()
-        for dev in [self.xn, self.yn, self.pair] + self.zn[1:]:
+        for dev in [self.plane_peer(i) for i in range(1, 8)] + self.zn[1:]:
             pl.semaphore_signal(sem, inc=1, device_id=dev, device_id_type=MESH)
-        pl.semaphore_wait(sem, 6)
+        pl.semaphore_wait(sem, 10)
 
 
 def remote(src, dst, send, recv, dev):
@@ -589,13 +593,20 @@
             col = self.col(x * 2 + self.p.c)
 
             def one(j, _, x=x, col=col):
-                i, d = j // 8, j % 8
-                mine = self.g[i, d // 2, d % 2, :, col].astype(F32)
-                theirs = self.held[x, i, d // 2, d % 2].astype(F32)
-                self.held[x, i, d // 2, d % 2] = (mine + theirs).astype(BF)
+                i, z = j // 4, j % 4
+                a = self.g[i, z, :, :, col].astype(F32) + self.held[x, i, z].astype(F32)
+                self.held[x, i, z] = a.astype(BF)
                 return 0
 
-            lax.fori_loop(0, self.n * 8, one, 0)
+            def whole(i, _, x=x, col=col):
+                a = self.g[i, :, :, :, col].astype(F32) + self.held[x, i].astype(F32)
+                self.held[x, i] = a.astype(BF)
+                return 0
+
+            if self.cols > 128:
+                lax.fori_loop(0, self.n * 4, one, 0)
+            else:
+                lax.fori_loop(0, self.n, whole, 0)
         self.corner_copy(0).start()
         self.corner_copy(1).start()
 
@@ -651,8 +662,8 @@
 
 
 class Tail:
-    def __init__(self, p, gt, hp, hx, hy, hz, out, ss, rs):
-        self.p, self.gt, self.hp, self.hx, self.hy, self.hz = p, gt, hp, hx, hy, hz
+    def __init__(self, p, gt, hp, hx, hy, hz, hc, out, ss, rs):
+        self.p, self.gt, self.hp, self.hx, self.hy, self.hz, self.hc = p, gt, hp, hx, hy, hz, hc
         self.out, self.ss, self.rs = out, ss, rs
 
     def cp(self, src, dst, i, dev):
@@ -662,7 +673,12 @@
         return self.cp(self.gt.at[j], self.hp.at[j // 2], j, self.p.pair)
 
     def x_copy(self, j):
-        return self.cp(self.gt.at[j], self.hx, 4, self.p.xn)
+        if j == 1:
+            return self.cp(self.gt.at[1, :, :, self.p.y], self.hx.at[:, :, 0], 4, self.p.xn)
+        return self.cp(self.gt.at[0], self.hx, 4, self.p.xn)
+
+    def corner_copy(self):
+        return self.cp(self.gt.at[1, :, :, 1 - self.p.y], self.hc, 9, self.p.yn)
 
     def y_copy(self, j):
         return self.cp(self.gt.at[j, :, :, 1 - self.p.y], self.hy, 5, self.p.yn)
@@ -680,34 +696,45 @@
     def sum_pair(self, j):
         def do():
             self.pair_copy(j).wait_recv()
-            if j >= 2:
-                self.x_copy(j).wait_recv()
-
-            def one(i, _):
-                w, d = i // 8, i % 8
-                at = (w, d // 2, d % 2)
-                a = self.gt[(j,) + at].astype(F32) + self.hp[(j // 2,) + at].astype(F32)
-                if j >= 2:
-                    a = a + self.hx[at].astype(F32)
-                self.gt[(j,) + at] = a.astype(BF)
-                return 0
-
-            lax.fori_loop(0, 24, one, 0)
-            if j < 2:
-                self.x_copy(j).start()
+            if j == 2:
+                self.x_copy(0).wait_recv()
+            for w in range(3):
+                a = self.gt[j, w].astype(F32) + self.hp[j // 2, w].astype(F32)
+                if j == 2:
+                    a = a + self.hx[w].astype(F32)
+                self.gt[j, w] = a.astype(BF)
+            if j == 0:
+                self.x_copy(0).start()
+            elif j == 1:
+                self.corner_copy().start()
             else:
                 self.y_copy(j).start()
 
         self.mine(j, do)
+
+    def corner(self):
+        def do():
+            self.corner_copy().wait_recv()
+            y = self.p.y
+            for w in range(3):
+                a = self.gt[1, w, :, y].astype(F32) + self.hc[w].astype(F32)
+                self.gt[1, w, :, y] = a.astype(BF)
+            self.x_copy(1).start()
+
+        self.mine(1, do)
 
     def sum_y(self, j):
         def do():
             p = self.p
             self.y_copy(j).wait_recv()
+            if j == 3:
+                self.x_copy(1).wait_recv()
             for i in range(3):
                 for k in (1, 2, 3):
                     zt = (p.z + k) % 4
                     a = self.gt[j, i, zt, p.y].astype(F32) + self.hy[i, zt].astype(F32)
+                    if j == 3:
+                        a = a + self.hx[i, zt, 0].astype(F32)
                     self.gt[j, i, zt, p.y] = a.astype(BF)
             for k in (1, 2, 3):
                 self.z_copy(j, k).start()
@@ -721,6 +748,8 @@
                 self.z_copy(j, k).wait_recv()
             for i in range(3):
                 a = self.gt[j, i, p.z, p.y].astype(F32) + self.hy[i, p.z].astype(F32)
+                if j == 3:
+                    a = a + self.hx[i, p.z, 0].astype(F32)
                 for k in range(3):
                     a = a + self.hz[k, i].astype(F32)
                 self.out[i] = a
@@ -733,6 +762,8 @@
 
         def sent(j):
             self.x_copy(j).wait_send()
+            if j == 1:
+                self.corner_copy().wait_send()
             self.y_copy(j + 2).wait_send()
             for k in (1, 2, 3):
                 self.z_copy(j + 2, k).wait_send()
@@ -843,8 +874,8 @@
         def out(i):
             rows = slice(i * 256, i * 256 + 256)
             if i < 2:
-                dk_own[rows, lanes] = dks[i] * 0.125
-                dv_own[rows, lanes] = dvs[i]
+                dk_own[rows, lanes] = (dks[i] * 0.125).astype(dk_own.dtype)
+                dv_own[rows, lanes] = dvs[i].astype(dv_own.dtype)
             else:
                 back = slice(i * 256 - 512, i * 256 - 256)
                 dkv_send[0, back, lanes] = (dks[i] * 0.125).astype(BF)
@@ -886,15 +917,16 @@
     sq, sk, sv, so, cq, ck, cv, co, up, down,
     g1, b1, g2, b2, g3, b3,
     y_o, dx_o, eg_o, ga_o, gb_o, gf_o, ns_o, vs_o,
-    x, enc, og, codes, wa, wb, wf, gt,
+    xs, enc, og, codes, wa, wb, wf, gt,
     q1, qt1, k1, v1, vt1, o1, ot1, l1,
     q2, qt2, k2, v2, vt2, o2, ot2, l2,
     bias, n1, n2, h1b, h2b, u, gp, dg, dz, low, lowt, do, dot_,
     kvs, kvr1, kvr2, tt, yb, row, st,
-    hc, hq, hu, hd, c1, c2, c3, p1, p2, p3, u1, u2, u3, d1, d2, d3, hp, hx, hy, hz,
+    hc, hq, hu, hd, c1, c2, c3, p1, p2, p3, u1, u2, u3, d1, d2, d3, hp, hx, hy, hz, hcn,
     st_r, gss, grs, rss, rrs, aas, ars, ess, ers, tss, trs, ls,
 ):
     dqt, dq = h2b, q2
+    x = xs.at[pl.ds(0, 512)]
     dkv = [v2.at[pl.ds(0, 512)], v2.at[pl.ds(512, 512)]]
     p = Place()
     loads = []
@@ -924,6 +956,10 @@
     GA.oxy()
     for cp in loads[3:]:
         cp.wait()
+    halves = remote(
+        xs.at[pl.ds(0, 512)], xs.at[pl.ds(512, 512)], ess.at[9], ers.at[9], p.pair
+    )
+    halves.start()
     GB.oxy()
 
     def mat(w, j):
@@ -946,7 +982,6 @@
             c = code[j * 128 : j * 128 + 128, :1]
             ok = (c >= base) & (c <= high)
             bias[i * 512 + j * 128 : i * 512 + j * 128 + 128, :] = jnp.where(ok, 0.0, -2.0e9)
-    tt[...] = turn(x[...])
 
     GA.plane(GB.zs)
     GU.oxy()
@@ -958,21 +993,19 @@
     GA.finish()
     GD.zs()
 
-    xv = x[...]
-    k1[0:512, :] = nn(xv, mat(wa, 1)).astype(BF)
-    v1[0:512, :] = nn(xv, mat(wa, 2)).astype(BF)
-
     def swap(buf, i):
         return remote(buf.at[pl.ds(0, 512)], buf.at[pl.ds(512, 512)], ess.at[i], ers.at[i], p.pair)
 
-    swap(k1, 0).start()
-    swap(v1, 1).start()
+    halves.wait()
+    xv = xs[...]
+    k1[...] = nn(xv, mat(wa, 1)).astype(BF)
+    vv = nn(xv, mat(wa, 2)).astype(BF)
+    v1[...] = vv
+    vt1[...] = turn(vv)
+    xv = x[...]
     qv = nn(xv, mat(wa, 0)).astype(BF)
     q1[...] = qv
     qt1[...] = turn(qv)
-    swap(k1, 0).wait_recv()
-    swap(v1, 1).wait_recv()
-    vt1[...] = turn(v1[...])
     attend(qt1, k1, vt1, bias, ot1, l1, gp, {(0, 0): GB.corner, (1, 0): GU.plane, (2, 0): GB.cross, (3, 0): GD.plane})
     o1[...] = turn(ot1[...].astype(BF))
     GB.finish()
@@ -1098,12 +1131,12 @@
     RU.corner()
     attend_back(
         q2, qt2, k2, vt2, v2, do, dot_, ot2, None, l2, dqt,
-        gp.at[pl.ds(0, 512)], gp.at[pl.ds(512, 512)], kvs, lambda step: step,
+        gp.at[pl.ds(0, 512)], gp.at[pl.ds(512, 512)], kvs.at[:, pl.ds(512, 512)], lambda step: step,
         {(0, 0): RD.plane, (1, 0): RU.plane, (3, 0): RD.along},
     )
 
     def swap_back(buf, i):
-        return remote(kvs, buf, ess.at[i], ers.at[i], p.pair)
+        return remote(kvs.at[:, pl.ds(512, 512)], buf, ess.at[i], ers.at[i], p.pair)
 
     swap_back(kvr2, 4).start()
     dqv = turn(dqt[...])
@@ -1112,7 +1145,7 @@
     wb[2] = nn(tt[...], dqv).astype(BF).reshape(4, 2, 64, 512)
     tt[...] = turn(enc[...])
     swap_back(kvr2, 4).wait()
-    for i in range(4):
+    for i in (2, 3):
         swap((k1, v1, k2, v2)[i], i).wait_send()
 
     def join(recv, at):
@@ -1151,8 +1184,8 @@
     RC.start()
     RP.corner()
     vt1[...] = turn(k1[...])
-    tt[...] = turn(x[...])
-    T = Tail(p, gt, hp, hx, hy, hz, ga_o, aas, ars)
+    vt2[...] = turn(xs[...])
+    T = Tail(p, gt, hp, hx, hy, hz, hcn, ga_o, aas, ars)
 
     def order(step):
         far = (step // 2) * p.x + (1 - step // 2) * (1 - p.x)
@@ -1164,24 +1197,16 @@
     def part_back(step):
         at = lanes_of(step)
         return remote(
-            kvs.at[:, :, at], kvr1.at[:, :, at], ess.at[5 + step], ers.at[5 + step], p.pair
+            kvs.at[:, pl.ds(512, 512), at], kvr1.at[:, :, at], ess.at[5 + step], ers.at[5 + step], p.pair
         )
 
     def grads(step):
         at = lanes_of(step)
-        part_back(step).wait_recv()
-
-        def one(r):
-            for i in (0, 1):
-                rows = pl.ds(pl.multiple_of(r.start + 1024 + i * 512, CH), CH)
-                dkv[i][r, at] = (gp[rows, at] + kvr1[i, r, at].astype(F32)).astype(BF)
-
-        row_steps(512, one)
         dqv = turn(dqt[at, :])
         dq[:, at] = dqv
-        gt[step, 0] = nn(tt[...], dqv).astype(BF).reshape(4, 2, 64, 128)
-        gt[step, 1] = nn(tt[...], dkv[0][:, at]).astype(BF).reshape(4, 2, 64, 128)
-        gt[step, 2] = nn(tt[...], dkv[1][:, at]).astype(BF).reshape(4, 2, 64, 128)
+        gt[step, 0] = nn(vt2[:, 0:512], dqv).astype(BF).reshape(4, 2, 64, 128)
+        gt[step, 1] = nn(vt2[...], kvs[0, :, at]).astype(BF).reshape(4, 2, 64, 128)
+        gt[step, 2] = nn(vt2[...], kvs[1, :, at]).astype(BF).reshape(4, 2, 64, 128)
         T.start(step)
 
     def both(*fns):
@@ -1193,23 +1218,31 @@
 
     attend_back(
         q1, qt1, k1, vt1, v1, do, dot_, ot1, bias, l1, dqt,
-        gp.at[pl.ds(1024, 512)], gp.at[pl.ds(1536, 512)], kvs, order,
+        kvs.at[0, pl.ds(0, 512)], kvs.at[1, pl.ds(0, 512)], kvs.at[:, pl.ds(512, 512)], order,
         {
             (0, 0): RC.corner,
-            (0, 1): both(lambda: part_back(0).start(), RP.plane),
-            (1, 0): lambda: grads(0),
-            (1, 1): both(lambda: part_back(1).start(), RC.plane, RD.finish),
-            (2, 0): both(lambda: grads(1), lambda: T.sum_pair(0)),
-            (2, 1): both(lambda: part_back(2).start(), RP.along, RU.finish),
-            (3, 0): both(lambda: grads(2), lambda: T.sum_pair(1)),
-            (3, 1): both(lambda: part_back(3).start(), RC.along),
+            (0, 1): both(lambda: part_back(0).start(), lambda: grads(0), RP.plane),
+            (1, 0): lambda: T.sum_pair(0),
+            (1, 1): both(lambda: part_back(1).start(), lambda: grads(1), RC.plane, RD.finish),
+            (2, 0): lambda: T.sum_pair(1),
+            (2, 1): both(lambda: part_back(2).start(), lambda: grads(2), RP.along, RU.finish),
+            (3, 0): lambda: T.sum_pair(2),
+            (3, 1): both(lambda: part_back(3).start(), T.corner, RC.along),
         },
     )
-    T.sum_pair(2)
     grads(3)
+    T.sum_y(2)
+    dz[...] += nt(dq[...], mat(wa, 0))
+    for step in range(4):
+        part_back(step).wait_recv()
+
+    def join_last(r):
+        for i in (0, 1):
+            dkv[i][r, :] = (kvs[i, r, :].astype(F32) + kvr1[i, r, :].astype(F32)).astype(BF)
+
+    row_steps(512, join_last)
     T.sum_pair(3)
-    T.sum_y(2)
-    dz[...] += nt(dq[...], mat(wa, 0)) + nt(dkv[0][...], mat(wa, 1)) + nt(dkv[1][...], mat(wa, 2))
+    dz[...] += nt(dkv[0][...], mat(wa, 1)) + nt(dkv[1][...], mat(wa, 2))
     x_copy = pltpu.make_async_copy(dz, dx_o, ls.at[1])
     x_copy.start()
 
@@ -1218,35 +1251,36 @@
 
     row_steps(512, squares)
 
-    def stat(i, src, dev):
-        return remote(src, st_r.at[i], tss.at[i], trs.at[i], dev)
-
-    stat(0, st, p.pair).start()
+    stats = []
+    st_r[0] = st[...]
+    for i in range(1, 8):
+        stats.append(remote(st, st_r.at[i], tss.at[i], trs.at[i], p.plane_peer(i)))
+    for cp in stats:
+        cp.start()
     T.sum_y(3)
-    stat(0, st, p.pair).wait()
-    st_r[6] = st[...] + st_r[0]
-    stat(1, st_r.at[6], p.xn).start()
-    T.finish(2)
+    for cp in stats:
+        cp.wait()
+    total = None
+    for i in range(8):
+        x, y, c = (p.x + i // 4) % 2, (p.y + i // 2) % 2, (p.c + i) % 2
+        part = st_r[x * 4 + y * 2 + c]
+        total = part if total is None else total + part
+    st_r[8 + p.z] = total
+    stats = []
+    for k in (1, 2, 3):
+        at = st_r.at[8 + p.z]
+        stats.append((remote(at, at, tss.at[7 + k], trs.at[7 + k], p.zn[k]), k))
+    for cp, _ in stats:
+        cp.start()
     RP.finish()
     RC.finish()
-    stat(1, st_r.at[6], p.xn).wait()
-    st_r[7] = st_r[6] + st_r[1]
-    stat(2, st_r.at[7], p.yn).start()
-    stat(2, st_r.at[7], p.yn).wait()
-    st_r[8] = st_r[7] + st_r[2]
-    for k in (1, 2, 3):
-        stat(2 + k, st_r.at[8], p.zn[k]).start()
+    T.finish(2)
+    for cp, k in stats:
+        cp.wait_send()
+        back = st_r.at[8 + (p.z - k + 4) % 4]
+        remote(back, back, tss.at[7 + k], trs.at[7 + k], p.zn[k]).wait_recv()
     T.finish(3)
-    for k in (1, 2, 3):
-        stat(2 + k, st_r.at[8], p.zn[k]).wait()
-    total = None
-    for zs in range(4):
-        part = None
-        for k in range(4):
-            got = st_r[8] if k == 0 else st_r[2 + k]
-            got = jnp.where((p.z - k + 4) % 4 == zs, got, 0.0)
-            part = got if part is None else part + got
-        total = part if total is None else total + part
+    total = st_r[8] + st_r[9] + st_r[10] + st_r[11]
     ns_o[...] = total[0:6]
     vs_o[...] = jnp.sqrt(total[6:8] * (1.0 / 16384.0))
     for step in range(4):
@@ -1310,7 +1344,7 @@
         ]
 
     scratch = (
-        [V(512, 512)] * 3
+        [V(1024, 512), V(512, 512), V(512, 512)]
         + [V(8, 1024, dtype=jnp.int32)]
         + [V(3, 4, 2, 64, 512), V(5, 4, 2, 64, 512), V(2, 4, 2, 64, 2048), V(4, 3, 4, 2, 64, 128)]
         + attention()
@@ -1319,13 +1353,13 @@
         + [V(512, 512), V(512, 512)]
         + [V(512, 2048), V(2048, 512, dtype=F32), V(512, 2048), V(512, 512, dtype=F32)]
         + [V(512, 512)] * 4
-        + [V(2, 512, 512), V(2, 512, 512), V(2, 512, 512)]
+        + [V(2, 1024, 512), V(2, 512, 512), V(2, 512, 512)]
         + [V(512, 512), V(512, 512, dtype=F32), V(512, 128, dtype=F32), V(8, 512, dtype=F32)]
         + [rc[0], rp[0], ru[0], rd[0]]
         + rc[1] + rp[1] + ru[1] + rd[1]
-        + [V(2, 3, 4, 2, 64, 128), V(3, 4, 2, 64, 128), V(3, 4, 64, 128), V(3, 3, 64, 128)]
-        + [V(9, 8, 512, dtype=F32)]
-        + [S(4, 19), S(4, 19), S(4, 9), S(4, 9), S(9), S(9), S(9), S(9), S(6), S(6), S(13)]
+        + [V(2, 3, 4, 2, 64, 128), V(3, 4, 2, 64, 128), V(3, 4, 64, 128), V(3, 3, 64, 128), V(3, 4, 64, 128)]
+        + [V(12, 8, 512, dtype=F32)]
+        + [S(4, 19), S(4, 19), S(4, 9), S(4, 9), S(10), S(10), S(10), S(10), S(11), S(11), S(13)]
     )
     big = jax.ShapeDtypeStruct((512, 512), F32)
     outs = pl.pallas_call(

time: 123 us -> 117 us (0.951)
  Pallas kernels: 122 us -> 116 us
    pallas_call x1, Pallas kernels: 118 us -> 112 us  [fast_shards(): pl.pallas_call(fast_kernel, out_shape=[big, big, big] + [jax.ShapeDtypeSt...]
where the time goes in v4:
time: 117 us
  Pallas kernels  116 us (99%)
    pallas_call x1, Pallas kernels, fast_shards(): pl.pallas_call(fast_kernel, out_shape=[big, big, big] + [jax.ShapeDtypeSt...  112 us
    pallas_call x1, Pallas kernels, fast_shards(): pl.pallas_call(place_kernel, out_shape=ends, in_specs=[hbm] * 8, out_spec...  3.49 us

profile of v4, /device:TPU:0, one launch (start us, length us, event | category | flops | bytes accessed | tf_op | source)
XLA Modules:
  0.0 116.5 jit_solution(5001371225338824387)
XLA Ops:
  0.7 112.2 %layer.1 = (f32[512,512]{1,0:T(8,128)}, f32[512,512]{1,0:T(8,128)}, f32[512,512]{1,0:T(8,128)}, f32[3,64,128]{2,1,0:T(8,128)}, f32[5,64,128]{2,1,0:T(8,128)}, /*...) custom-call(bf16[512,512]{1,0:T(8,128)(2,1)} %x_i.1, bf16[512,512]{1,0:T(8,128)(2,1)} %enc_i.1, ...), custom_call_target="tpu_custom_call" | custom-call | tf_op jit(solution)/shard_map/layer/pallas_call | solution.py:1365
  112.8 3.5 %place.1 = (f32[512,512]{1,0:T(8,128)}, f32[512,512]{1,0:T(8,128)}, f32[512,512]{1,0:T(8,128)}, f32[64,128]{1,0:T(8,128)}, f32[64,128]{1,0:T(8,128)}, /*index=5*...) custom-call(f32[512,512]{1,0:T(8,128)} %get-tuple-element.38.refs_0_, ...), custom_call_target="tpu_custom_call" | custom-call | tf_op jit(solution)/shard_map/place/pallas_call | solution.py:1384

commit v5 on v4

--- a/solution.py
+++ b/solution.py
@@ -402,7 +402,7 @@
 F32 = jnp.float32
 LOG2E = 1.4426950408889634
 SCALE = 0.125 * LOG2E
-CH = 256
+CH = 512
 
 
 def nn(a, b):
@@ -1084,9 +1084,6 @@
     y_copy.start()
     lv = low[...]
     lowt[...] = turn(lv)
-    for j in range(4):
-        cols = slice(j * 512, j * 512 + 512)
-        dg[:, cols] = (nn(lv, wf[1, :, :, :, cols].reshape(512, 512)) * gp[cols, :]).astype(BF)
     for g in G:
         g.drain()
     RC, RP, RU, RD = R = [
@@ -1102,8 +1099,10 @@
     ]
     for j in range(4):
         cols = slice(j * 512, j * 512 + 512)
+        dg[:, cols] = (nn(lv, wf[1, :, :, :, cols].reshape(512, 512)) * gp[cols, :]).astype(BF)
         wf[1, :, :, :, cols] = nn(lowt[...], u[:, cols]).astype(BF).reshape(4, 2, 64, 512)
-    RD.start()
+        if j % 2 == 1:
+            RD.pair_copy(j // 2).start()
     dz[...] += nt(dg[...], mat(wf, 0))
     tt[...] = turn(h2b[...])
     for j in range(4):

time: 117 us -> 115 us (0.983)
  Pallas kernels: 116 us -> 114 us
    pallas_call x1, Pallas kernels: 112 us -> 110 us  [fast_shards(): pl.pallas_call(fast_kernel, out_shape=[big, big, big] + [jax.ShapeDtypeSt...]
where the time goes in v5:
time: 115 us
  Pallas kernels  114 us (99%)
    pallas_call x1, Pallas kernels, fast_shards(): pl.pallas_call(fast_kernel, out_shape=[big, big, big] + [jax.ShapeDtypeSt...  110 us
    pallas_call x1, Pallas kernels, fast_shards(): pl.pallas_call(place_kernel, out_shape=ends, in_specs=[hbm] * 8, out_spec...  3.49 us

profile of v5, /device:TPU:0, one launch (start us, length us, event | category | flops | bytes accessed | tf_op | source)
XLA Modules:
  0.0 114.7 jit_solution(199251752595678466)
XLA Ops:
  0.7 110.3 %layer.1 = (f32[512,512]{1,0:T(8,128)}, f32[512,512]{1,0:T(8,128)}, f32[512,512]{1,0:T(8,128)}, f32[3,64,128]{2,1,0:T(8,128)}, f32[5,64,128]{2,1,0:T(8,128)}, /*...) custom-call(bf16[512,512]{1,0:T(8,128)(2,1)} %x_i.1, bf16[512,512]{1,0:T(8,128)(2,1)} %enc_i.1, ...), custom_call_target="tpu_custom_call" | custom-call | tf_op jit(solution)/shard_map/layer/pallas_call | solution.py:1364
  111.0 3.5 %place.1 = (f32[512,512]{1,0:T(8,128)}, f32[512,512]{1,0:T(8,128)}, f32[512,512]{1,0:T(8,128)}, f32[64,128]{1,0:T(8,128)}, f32[64,128]{1,0:T(8,128)}, /*index=5*...) custom-call(f32[512,512]{1,0:T(8,128)} %get-tuple-element.38.refs_0_, ...), custom_call_target="tpu_custom_call" | custom-call | tf_op jit(solution)/shard_map/place/pallas_call | solution.py:1383

commit v6 on v5

--- a/solution.py
+++ b/solution.py
@@ -1008,6 +1008,7 @@
     qt1[...] = turn(qv)
     attend(qt1, k1, vt1, bias, ot1, l1, gp, {(0, 0): GB.corner, (1, 0): GU.plane, (2, 0): GB.cross, (3, 0): GD.plane})
     o1[...] = turn(ot1[...].astype(BF))
+    vt1[...] = turn(k1[...])
     GB.finish()
     ev = enc[...]
     k2[0:512, :] = nn(ev, mat(wb, 3)).astype(BF)
@@ -1032,6 +1033,7 @@
     vt2[...] = turn(v2[...])
     attend(qt2, k2, vt2, None, ot2, l2, gp, {(0, 1): GD.corner, (2, 1): GU.cross})
     o2[...] = turn(ot2[...].astype(BF))
+    vt2[...] = turn(k2[...])
     yb[...] = nt(o2[...], mat(wb, 1))
 
     def second(r):
@@ -1041,6 +1043,7 @@
         h2b[r, :] = (n * g2[...] + b2[...]).astype(BF)
 
     row_steps(512, second)
+    tt[...] = turn(h2b[...])
     hv = h2b[...]
     blocks = [p.t, p.pair[1], p.xt, (1 - p.x) * 2 + 1 - p.c]
     waits = [None, GU.p_recv(0).wait_recv, GD.cross, GU.p_recv(1).wait_recv]
@@ -1104,7 +1107,6 @@
         if j % 2 == 1:
             RD.pair_copy(j // 2).start()
     dz[...] += nt(dg[...], mat(wf, 0))
-    tt[...] = turn(h2b[...])
     for j in range(4):
         cols = slice(j * 512, j * 512 + 512)
         wf[0, :, :, :, cols] = nn(tt[...], dg[:, cols]).astype(BF).reshape(4, 2, 64, 512)
@@ -1126,7 +1128,6 @@
     dot_[...] = turn(dov)
     lowt[...] = turn(low[...])
     wb[1] = nn(lowt[...], o2[...]).astype(BF).reshape(4, 2, 64, 512)
-    vt2[...] = turn(k2[...])
     RU.corner()
     attend_back(
         q2, qt2, k2, vt2, v2, do, dot_, ot2, None, l2, dqt,
@@ -1182,7 +1183,6 @@
     wb[0] = nn(lowt[...], o1[...]).astype(BF).reshape(4, 2, 64, 512)
     RC.start()
     RP.corner()
-    vt1[...] = turn(k1[...])
     vt2[...] = turn(xs[...])
     T = Tail(p, gt, hp, hx, hy, hz, hcn, ga_o, aas, ars)
 

time: 115 us -> 115 us (level)
  no operation moved by 1% of the time
where the time goes in v6:
time: 115 us; the launch traced here: 114 us
  Pallas kernels  113 us (98%)
    pallas_call x1, Pallas kernels, fast_shards(): pl.pallas_call(fast_kernel, out_shape=[big, big, big] + [jax.ShapeDtypeSt...  110 us
    pallas_call x1, Pallas kernels, fast_shards(): pl.pallas_call(place_kernel, out_shape=ends, in_specs=[hbm] * 8, out_spec...  3.49 us

profile of v6, /device:TPU:0, one launch (start us, length us, event | category | flops | bytes accessed | tf_op | source)
XLA Modules:
  0.0 114.1 jit_solution(22509660195113465)
XLA Ops:
  0.7 109.7 %layer.1 = (f32[512,512]{1,0:T(8,128)}, f32[512,512]{1,0:T(8,128)}, f32[512,512]{1,0:T(8,128)}, f32[3,64,128]{2,1,0:T(8,128)}, f32[5,64,128]{2,1,0:T(8,128)}, /*...) custom-call(bf16[512,512]{1,0:T(8,128)(2,1)} %x_i.1, bf16[512,512]{1,0:T(8,128)(2,1)} %enc_i.1, ...), custom_call_target="tpu_custom_call" | custom-call | tf_op jit(solution)/shard_map/layer/pallas_call | solution.py:1364
  110.4 3.5 %place.1 = (f32[512,512]{1,0:T(8,128)}, f32[512,512]{1,0:T(8,128)}, f32[512,512]{1,0:T(8,128)}, f32[64,128]{1,0:T(8,128)}, f32[64,128]{1,0:T(8,128)}, /*index=5*...) custom-call(f32[512,512]{1,0:T(8,128)} %get-tuple-element.38.refs_0_, ...), custom_call_target="tpu_custom_call" | custom-call | tf_op jit(solution)/shard_map/place/pallas_call | solution.py:1383

commit v7 on v6

--- a/solution.py
+++ b/solution.py
@@ -1232,6 +1232,7 @@
     grads(3)
     T.sum_y(2)
     dz[...] += nt(dq[...], mat(wa, 0))
+    T.sum_pair(3)
     for step in range(4):
         part_back(step).wait_recv()
 
@@ -1240,7 +1241,6 @@
             dkv[i][r, :] = (kvs[i, r, :].astype(F32) + kvr1[i, r, :].astype(F32)).astype(BF)
 
     row_steps(512, join_last)
-    T.sum_pair(3)
     dz[...] += nt(dkv[0][...], mat(wa, 1)) + nt(dkv[1][...], mat(wa, 2))
     x_copy = pltpu.make_async_copy(dz, dx_o, ls.at[1])
     x_copy.start()

time: 115 us -> 115 us (level)
  no operation moved by 1% of the time
where the time goes in v7:
time: 115 us; the launch traced here: 114 us
  Pallas kernels  113 us (98%)
    pallas_call x1, Pallas kernels, fast_shards(): pl.pallas_call(fast_kernel, out_shape=[big, big, big] + [jax.ShapeDtypeSt...  110 us
    pallas_call x1, Pallas kernels, fast_shards(): pl.pallas_call(place_kernel, out_shape=ends, in_specs=[hbm] * 8, out_spec...  3.49 us

profile of v7, /device:TPU:0, one launch (start us, length us, event | category | flops | bytes accessed | tf_op | source)
XLA Modules:
  0.0 114.2 jit_solution(15791559119260141589)
XLA Ops:
  0.7 109.9 %layer.1 = (f32[512,512]{1,0:T(8,128)}, f32[512,512]{1,0:T(8,128)}, f32[512,512]{1,0:T(8,128)}, f32[3,64,128]{2,1,0:T(8,128)}, f32[5,64,128]{2,1,0:T(8,128)}, /*...) custom-call(bf16[512,512]{1,0:T(8,128)(2,1)} %x_i.1, bf16[512,512]{1,0:T(8,128)(2,1)} %enc_i.1, ...), custom_call_target="tpu_custom_call" | custom-call | tf_op jit(solution)/shard_map/layer/pallas_call | solution.py:1364
  110.5 3.5 %place.1 = (f32[512,512]{1,0:T(8,128)}, f32[512,512]{1,0:T(8,128)}, f32[512,512]{1,0:T(8,128)}, f32[64,128]{1,0:T(8,128)}, f32[64,128]{1,0:T(8,128)}, /*index=5*...) custom-call(f32[512,512]{1,0:T(8,128)} %get-tuple-element.38.refs_0_, ...), custom_call_target="tpu_custom_call" | custom-call | tf_op jit(solution)/shard_map/place/pallas_call | solution.py:1383
